TPU v7x, 32 devices: a whole 2x2x4 slice. The times are simulated.
32 devices in a mesh: ctx: 8 (over y, x, core), fsdp: 4 (over z).
Axes of the slice: x: 2, y: 2, z: 4, core: 2. Of those that a mesh axis runs over, the one named last changes fastest.
Arguments:
- block_input: bfloat16 [4096, 768], P(('ctx', 'fsdp')), may hold values from -6 to 6
- positions: int32 [4096], replicated, may hold values from 0 to 4095, as said below
- norm1_gain: bfloat16 [768], P('fsdp'), may hold values from 0.5 to 1.5
- norm1_bias: bfloat16 [768], P('fsdp'), may hold values from -3 to 3
- qkv_weight: bfloat16 [768, 2304], P('fsdp'), may hold values from -0.21875 to 0.21875
- query_bias: bfloat16 [768], P('fsdp'), may hold values from -3 to 3
- value_bias: bfloat16 [768], P('fsdp'), may hold values from -3 to 3
- proj_weight: bfloat16 [768, 768], P('fsdp'), may hold values from -1.75 to 1.75
- proj_bias: bfloat16 [768], P('fsdp'), may hold values from -3 to 3
- norm2_gain: bfloat16 [768], P('fsdp'), may hold values from 0.5 to 1.5
- norm2_bias: bfloat16 [768], P('fsdp'), may hold values from -3 to 3
- fc_weight: bfloat16 [768, 3072], P('fsdp'), may hold values from -0.21875 to 0.21875
- fc_bias: bfloat16 [3072], P('fsdp'), may hold values from -3 to 3
- out_weight: bfloat16 [3072, 768], P('fsdp'), may hold values from -0.109375 to 0.109375
- out_bias: bfloat16 [768], P('fsdp'), may hold values from -3 to 3
- cotangent: bfloat16 [4096, 768], P(('ctx', 'fsdp')), may hold values from -6 to 6
Outputs:
- block_output: float32 [4096, 768], P(('ctx', 'fsdp'))
- input_grad: float32 [4096, 768], P(('ctx', 'fsdp'))
- norm1_gain_grad: float32 [768], P('fsdp')
- norm1_bias_grad: float32 [768], P('fsdp')
- qkv_weight_grad: float32 [768, 2304], P('fsdp')
- query_bias_grad: float32 [768], P('fsdp')
- value_bias_grad: float32 [768], P('fsdp')
- proj_weight_grad: float32 [768, 768], P('fsdp')
- proj_bias_grad: float32 [768], P('fsdp')
- norm2_gain_grad: float32 [768], P('fsdp')
- norm2_bias_grad: float32 [768], P('fsdp')
- fc_weight_grad: float32 [768, 3072], P('fsdp')
- fc_bias_grad: float32 [3072], P('fsdp')
- out_weight_grad: float32 [3072, 768], P('fsdp')
- out_bias_grad: float32 [768], P('fsdp')
Inputs may be any that keep to these rules, and one draw needn't show every extreme that they name: positions is a permutation of 0 to 4095. For every g, the entries 2 * 256 * g to 2 * 256 * (g + 1) - 1 hold the 256 positions of a sequence block b_g in increasing order, then those of block 15 - b_g in increasing order; the b_g over all g are the numbers 0 to 7 in an order drawn from the seed.
All inputs are finite; a program needn't handle non-finite values.
Results may differ from a plain program's by a relative error of at most 0.03.
Values may be sent and summed in bfloat16 or wider, within the bound.
A program may use at most 128 MiB of HBM per device.

v0:
```python
import jax
import jax.numpy as jnp
from jax import lax
from jax.sharding import PartitionSpec as P

HEADS = 12
HEAD = 64


EPSILON = 1e-05
NEG_FILL = -1e30
GELU_C = 0.7978845608028654
GELU_K = 0.044715


def passed_along(block, axis, distance):
    devices = range(lax.axis_size(axis))
    route = [((i - distance) % len(devices), i) for i in devices]
    return lax.ppermute(block, axis, route)


def layer_norm(values_in, gain, shift):
    row_mean = jnp.mean(values_in, axis=-1, keepdims=True)
    centered = values_in - row_mean
    variance = jnp.mean(centered * centered, axis=-1, keepdims=True)
    inv_std = lax.rsqrt(variance + EPSILON)
    normed = centered * inv_std
    return (normed * gain.astype(jnp.float32) + shift.astype(jnp.float32), normed, inv_std)


def norm_backward(grad_norm, gain, normed, inv_std):
    scaled = grad_norm * gain.astype(jnp.float32)
    scaled_mean = jnp.mean(scaled, axis=-1, keepdims=True)
    cross_mean = jnp.mean(scaled * normed, axis=-1, keepdims=True)
    return inv_std * (scaled - scaled_mean - normed * cross_mean)


def gelu_forward(pre_act):
    cubed = pre_act * pre_act * pre_act
    return 0.5 * pre_act * (1.0 + jnp.tanh(GELU_C * (pre_act + GELU_K * cubed)))


def gelu_slope(pre_act):
    cubed = pre_act * pre_act * pre_act
    tanh_value = jnp.tanh(GELU_C * (pre_act + GELU_K * cubed))
    return 0.5 * (1.0 + tanh_value) + 0.5 * pre_act * (1.0 - tanh_value * tanh_value) * GELU_C * (
        1.0 + 3.0 * GELU_K * pre_act * pre_act
    )


def rows_product(left, right):
    return lax.dot_general(
        left, right, (((0,), (0,)), ((), ())), preferred_element_type=jnp.float32
    )


def transposed_product(left, right):
    return lax.dot_general(
        left, right, (((1,), (1,)), ((), ())), preferred_element_type=jnp.float32
    )


def split_heads(matrix):
    return matrix.reshape(matrix.shape[0], HEADS, HEAD)


def masked_scores(query, query_pos, keys, key_pos):
    scores = jnp.einsum(
        "rhd,khd->hrk", split_heads(query), split_heads(keys), preferred_element_type=jnp.float32
    ) * HEAD ** (-0.5)
    allowed = (key_pos[None, :] <= query_pos[:, None])[None]
    return (jnp.where(allowed, scores, NEG_FILL), allowed)


def attend_block(carried, query, query_pos, keys, values, key_pos):
    weighted, run_max, row_total = carried
    scores, allowed = masked_scores(query, query_pos, keys, key_pos)
    new_max = jnp.maximum(run_max, jnp.max(scores, axis=-1))
    weights = jnp.where(allowed, jnp.exp(scores - new_max[..., None]), 0.0)
    factor = jnp.exp(run_max - new_max)
    row_total = row_total * factor + jnp.sum(weights, axis=-1)
    update = jnp.einsum(
        "hrk,khd->rhd",
        weights,
        split_heads(values).astype(jnp.float32),
        precision=lax.Precision.HIGHEST,
        preferred_element_type=jnp.float32,
    )
    weighted = weighted * factor.T[:, :, None] + update
    return (weighted, new_max, row_total)


def attend_tile(carried, query, query_pos, keys, values, key_pos):
    half_rows = keys.shape[0] // 2
    latest = jnp.max(query_pos)
    for half_index in range(2):
        first_row = half_index * half_rows
        part_keys = keys[first_row : first_row + half_rows]
        part_values = values[first_row : first_row + half_rows]
        part_pos = key_pos[first_row : first_row + half_rows]

        def keep_state(state_in, block_keys, block_values, block_pos):
            return state_in

        def update_state(state_in, block_keys, block_values, block_pos):
            return attend_block(state_in, query, query_pos, block_keys, block_values, block_pos)

        carried = lax.cond(
            jnp.min(part_pos) > latest,
            keep_state,
            update_state,
            carried,
            part_keys,
            part_values,
            part_pos,
        )
    return carried


def block_grads(query, grad_attn, row_lse, row_delta, query_pos, keys, values, key_pos):
    scores, allowed = masked_scores(query, query_pos, keys, key_pos)
    probs = jnp.where(allowed, jnp.exp(scores - row_lse[..., None]), 0.0)
    grad_heads = split_heads(grad_attn)
    grad_values = jnp.einsum(
        "hrk,rhd->khd", probs.astype(jnp.bfloat16), grad_heads, preferred_element_type=jnp.float32
    )
    grad_probs = jnp.einsum(
        "rhd,khd->hrk", grad_heads, split_heads(values), preferred_element_type=jnp.float32
    )
    grad_scores = (probs * (grad_probs - row_delta[..., None])).astype(jnp.bfloat16)
    scale = HEAD ** (-0.5)
    grad_query = (
        jnp.einsum(
            "hrk,khd->rhd", grad_scores, split_heads(keys), preferred_element_type=jnp.float32
        )
        * scale
    )
    grad_keys = (
        jnp.einsum(
            "hrk,rhd->khd", grad_scores, split_heads(query), preferred_element_type=jnp.float32
        )
        * scale
    )
    key_rows = keys.shape[0]
    return (grad_query, grad_keys.reshape(key_rows, -1), grad_values.reshape(key_rows, -1))


def tile_grads(query, grad_attn, row_lse, row_delta, query_pos, keys, values, key_pos):
    half_rows = keys.shape[0] // 2
    key_width = keys.shape[1]
    latest = jnp.max(query_pos)
    query_total = jnp.zeros((query.shape[0], HEADS, HEAD), jnp.float32)
    key_parts = []
    value_parts = []
    for half_index in range(2):
        first_row = half_index * half_rows
        part_keys = keys[first_row : first_row + half_rows]
        part_values = values[first_row : first_row + half_rows]
        part_pos = key_pos[first_row : first_row + half_rows]

        def skipped(block_keys, block_values, block_pos):
            return (
                jnp.zeros((query.shape[0], HEADS, HEAD), jnp.float32),
                jnp.zeros((half_rows, key_width), jnp.float32),
                jnp.zeros((half_rows, key_width), jnp.float32),
            )

        def computed(block_keys, block_values, block_pos):
            return block_grads(
                query, grad_attn, row_lse, row_delta, query_pos, block_keys, block_values, block_pos
            )

        step_query, step_keys, step_values = lax.cond(
            jnp.min(part_pos) > latest, skipped, computed, part_keys, part_values, part_pos
        )
        query_total = query_total + step_query
        key_parts.append(step_keys)
        value_parts.append(step_values)
    return (query_total, jnp.concatenate(key_parts, axis=0), jnp.concatenate(value_parts, axis=0))


def shards(
    block_input,
    positions,
    norm1_gain,
    norm1_bias,
    qkv_weight,
    query_bias,
    value_bias,
    proj_weight,
    proj_bias,
    norm2_gain,
    norm2_bias,
    fc_weight,
    fc_bias,
    out_weight,
    out_bias,
    cotangent,
):
    rows = block_input.shape[0]
    width = block_input.shape[1]
    ctx_size = lax.axis_size("ctx")
    shard_count = lax.axis_size("fsdp")
    ctx_index = lax.axis_index("ctx")
    shard_index = lax.axis_index("fsdp")
    group_rows = rows * shard_count

    def key_positions(source):
        return lax.dynamic_slice_in_dim(positions, source * group_rows, group_rows)

    gain_one, shift_one, qkv_full, qbias_full, vbias_full, proj_full, pbias_full = (
        lax.all_gather(norm1_gain, "fsdp", axis=0, tiled=True),
        lax.all_gather(norm1_bias, "fsdp", axis=0, tiled=True),
        lax.all_gather(qkv_weight, "fsdp", axis=0, tiled=True),
        lax.all_gather(query_bias, "fsdp", axis=0, tiled=True),
        lax.all_gather(value_bias, "fsdp", axis=0, tiled=True),
        lax.all_gather(proj_weight, "fsdp", axis=0, tiled=True),
        lax.all_gather(proj_bias, "fsdp", axis=0, tiled=True),
    )
    gain_two, shift_two, fc_full, fbias_full, out_full, obias_full = (
        lax.all_gather(norm2_gain, "fsdp", axis=0, tiled=True),
        lax.all_gather(norm2_bias, "fsdp", axis=0, tiled=True),
        lax.all_gather(fc_weight, "fsdp", axis=0, tiled=True),
        lax.all_gather(fc_bias, "fsdp", axis=0, tiled=True),
        lax.all_gather(out_weight, "fsdp", axis=0, tiled=True),
        lax.all_gather(out_bias, "fsdp", axis=0, tiled=True),
    )
    residual = block_input.astype(jnp.float32)
    normed1_out, normed1, inv_std1 = layer_norm(residual, gain_one, shift_one)
    norm1 = normed1_out.astype(jnp.bfloat16)
    qkv = jnp.dot(norm1, qkv_full, preferred_element_type=jnp.float32)
    query = (qkv[:, :width] + qbias_full.astype(jnp.float32)).astype(jnp.bfloat16)
    keys = qkv[:, width : 2 * width].astype(jnp.bfloat16)
    values = (qkv[:, 2 * width :] + vbias_full.astype(jnp.float32)).astype(jnp.bfloat16)
    group_keys, group_values = (
        lax.all_gather(keys, "fsdp", axis=0, tiled=True),
        lax.all_gather(values, "fsdp", axis=0, tiled=True),
    )
    own_qpos = lax.dynamic_slice_in_dim(
        positions, (ctx_index * shard_count + shard_index) * rows, rows
    )
    own_kpos = key_positions(ctx_index)
    initial = (
        jnp.zeros((rows, HEADS, HEAD), jnp.float32),
        jnp.full((HEADS, rows), NEG_FILL, jnp.float32),
        jnp.zeros((HEADS, rows), jnp.float32),
    )
    carried = attend_tile(initial, query, own_qpos, group_keys, group_values, own_kpos)

    def forward_hop(hop_index, loop_carry):
        state_now, cycle_keys, cycle_values = loop_carry
        cycle_keys, cycle_values = passed_along((cycle_keys, cycle_values), "ctx", 1)
        source = (ctx_index - hop_index) % ctx_size
        state_now = attend_tile(
            state_now, query, own_qpos, cycle_keys, cycle_values, key_positions(source)
        )
        return (state_now, cycle_keys, cycle_values)

    result = lax.fori_loop(1, ctx_size, forward_hop, (carried, group_keys, group_values))
    carried = result[0]
    weighted, run_max, row_total = carried
    attn = (weighted / row_total.T[:, :, None]).reshape(rows, width).astype(jnp.bfloat16)
    row_lse = run_max + jnp.log(row_total)
    middle = (
        residual
        + jnp.dot(attn, proj_full, preferred_element_type=jnp.float32)
        + pbias_full.astype(jnp.float32)
    )
    normed2_out, normed2, inv_std2 = layer_norm(middle, gain_two, shift_two)
    norm2 = normed2_out.astype(jnp.bfloat16)
    pre_act = jnp.dot(norm2, fc_full, preferred_element_type=jnp.float32) + fbias_full.astype(
        jnp.float32
    )
    act = gelu_forward(pre_act).astype(jnp.bfloat16)
    block_output = (
        middle
        + jnp.dot(act, out_full, preferred_element_type=jnp.float32)
        + obias_full.astype(jnp.float32)
    )
    grad_out = cotangent.astype(jnp.float32)
    out_weight_grad = rows_product(act, cotangent)
    out_bias_grad = jnp.sum(grad_out, axis=0)
    grad_act = transposed_product(cotangent, out_full)
    grad_pre = grad_act * gelu_slope(pre_act)
    fc_bias_grad = jnp.sum(grad_pre, axis=0)
    grad_pre_half = grad_pre.astype(jnp.bfloat16)
    fc_weight_grad = rows_product(norm2, grad_pre_half)
    grad_norm2 = transposed_product(grad_pre_half, fc_full)
    norm2_gain_grad = jnp.sum(grad_norm2 * normed2, axis=0)
    norm2_bias_grad = jnp.sum(grad_norm2, axis=0)
    grad_middle = grad_out + norm_backward(grad_norm2, gain_two, normed2, inv_std2)
    mlp_shares = (
        lax.psum_scatter(norm2_gain_grad, "fsdp", scatter_dimension=0, tiled=True),
        lax.psum_scatter(norm2_bias_grad, "fsdp", scatter_dimension=0, tiled=True),
        lax.psum_scatter(fc_weight_grad, "fsdp", scatter_dimension=0, tiled=True),
        lax.psum_scatter(fc_bias_grad, "fsdp", scatter_dimension=0, tiled=True),
        lax.psum_scatter(out_weight_grad, "fsdp", scatter_dimension=0, tiled=True),
        lax.psum_scatter(out_bias_grad, "fsdp", scatter_dimension=0, tiled=True),
    )
    proj_bias_grad = jnp.sum(grad_middle, axis=0)
    grad_middle_half = grad_middle.astype(jnp.bfloat16)
    proj_weight_grad = rows_product(attn, grad_middle_half)
    grad_attn = transposed_product(grad_middle_half, proj_full).astype(jnp.bfloat16)
    row_delta = jnp.sum(
        split_heads(grad_attn).astype(jnp.float32) * split_heads(attn).astype(jnp.float32), axis=-1
    ).T
    grad_query, grad_keys, grad_values = tile_grads(
        query, grad_attn, row_lse, row_delta, own_qpos, group_keys, group_values, own_kpos
    )

    def pass_key_grads(key_grads):
        return passed_along((key_grads[0], key_grads[1]), "ctx", 1)

    def backward_hop(hop_index, loop_carry):
        query_sum, key_grads, cycle_keys, cycle_values = loop_carry
        cycle_keys, cycle_values = passed_along((cycle_keys, cycle_values), "ctx", 1)
        key_grads = pass_key_grads(key_grads)
        source = (ctx_index - hop_index) % ctx_size
        step_query, step_keys, step_values = tile_grads(
            query,
            grad_attn,
            row_lse,
            row_delta,
            own_qpos,
            cycle_keys,
            cycle_values,
            key_positions(source),
        )
        return (
            query_sum + step_query,
            (key_grads[0] + step_keys, key_grads[1] + step_values),
            cycle_keys,
            cycle_values,
        )

    result = lax.fori_loop(
        1, ctx_size, backward_hop, (grad_query, (grad_keys, grad_values), group_keys, group_values)
    )
    grad_query = result[0]
    key_grads = pass_key_grads(result[1])
    own_key_grad, own_value_grad = (
        lax.psum_scatter(key_grads[0], "fsdp", scatter_dimension=0, tiled=True),
        lax.psum_scatter(key_grads[1], "fsdp", scatter_dimension=0, tiled=True),
    )
    grad_query_rows = grad_query.reshape(rows, width)
    query_bias_grad = jnp.sum(grad_query_rows, axis=0)
    value_bias_grad = jnp.sum(own_value_grad, axis=0)
    grad_qkv = jnp.concatenate([grad_query_rows, own_key_grad, own_value_grad], axis=1).astype(
        jnp.bfloat16
    )
    qkv_weight_grad = rows_product(norm1, grad_qkv)
    grad_norm1 = transposed_product(grad_qkv, qkv_full)
    norm1_gain_grad = jnp.sum(grad_norm1 * normed1, axis=0)
    norm1_bias_grad = jnp.sum(grad_norm1, axis=0)
    input_grad = grad_middle + norm_backward(grad_norm1, gain_one, normed1, inv_std1)
    attn_shares = (
        lax.psum_scatter(norm1_gain_grad, "fsdp", scatter_dimension=0, tiled=True),
        lax.psum_scatter(norm1_bias_grad, "fsdp", scatter_dimension=0, tiled=True),
        lax.psum_scatter(qkv_weight_grad, "fsdp", scatter_dimension=0, tiled=True),
        lax.psum_scatter(query_bias_grad, "fsdp", scatter_dimension=0, tiled=True),
        lax.psum_scatter(value_bias_grad, "fsdp", scatter_dimension=0, tiled=True),
        lax.psum_scatter(proj_weight_grad, "fsdp", scatter_dimension=0, tiled=True),
        lax.psum_scatter(proj_bias_grad, "fsdp", scatter_dimension=0, tiled=True),
    )
    totals = lax.psum(
        (
            attn_shares[0],
            attn_shares[1],
            attn_shares[2],
            attn_shares[3],
            attn_shares[4],
            attn_shares[5],
            attn_shares[6],
            mlp_shares[0],
            mlp_shares[1],
            mlp_shares[2],
            mlp_shares[3],
            mlp_shares[4],
            mlp_shares[5],
        ),
        "ctx",
    )
    return (
        block_output,
        input_grad,
        totals[0],
        totals[1],
        totals[2],
        totals[3],
        totals[4],
        totals[5],
        totals[6],
        totals[7],
        totals[8],
        totals[9],
        totals[10],
        totals[11],
        totals[12],
    )


def solution(mesh):
    in_specs = (
        P(("ctx", "fsdp"), None),
        P(),
        P("fsdp"),
        P("fsdp"),
        P("fsdp", None),
        P("fsdp"),
        P("fsdp"),
        P("fsdp", None),
        P("fsdp"),
        P("fsdp"),
        P("fsdp"),
        P("fsdp", None),
        P("fsdp"),
        P("fsdp", None),
        P("fsdp"),
        P(("ctx", "fsdp"), None),
    )
    out_specs = (
        P(("ctx", "fsdp"), None),
        P(("ctx", "fsdp"), None),
        P("fsdp"),
        P("fsdp"),
        P("fsdp", None),
        P("fsdp"),
        P("fsdp"),
        P("fsdp", None),
        P("fsdp"),
        P("fsdp"),
        P("fsdp"),
        P("fsdp", None),
        P("fsdp"),
        P("fsdp", None),
        P("fsdp"),
    )
    return jax.shard_map(shards, mesh=mesh, in_specs=in_specs, out_specs=out_specs, check_vma=False)
```

profile of v0, /device:TPU:0, one launch (start us, length us, event | category | flops | bytes accessed | tf_op | source)
XLA Modules:
  0.0 1640.0 jit_solution(4639262604445950894)
XLA Ops:
  13.3 21.9 %all-reduce.20 = (bf16[768]{0:T(1024)(128)(2,1)S(1)}, bf16[768]{0:T(1024)(128)(2,1)S(1)}, bf16[768]{0:T(1024)(128)(2,1)S(1)}, bf16[768]{0:T(1024)(128)(2,1)S(1)}...) all-reduce(bf16[768]{0:T(1024)(128)(2,1)S(1)} %dynamic-update-slice, ...), channel_id=1, replica_groups=mesh['ctx'=8,'fsdp'=4] {'fsdp'}, use_global_device_ids=true, to_apply=%add.1 | all-reduce | flops 6144 | bytes 24576
  41.8 13.8 all-gather
  57.7 25.0 %all-gather.6.cloned.1.call-done = bf16[768,2304]{1,0:T(8,128)(2,1)} async-done(((bf16[192,2304]{1,0:T(8,128)(2,1)}), bf16[768,2304]{1,0:T(8,128)(2,1)}) %all-gather.6.cloned.1.call-update) | async-done | bytes 3538960 | tf_op jit(solution)/shard_map/all_gather | solution.py:214
  85.5 25.9 %all_gather.49 = bf16[512,768]{1,0:T(8,128)(2,1)S(1)} all-gather(bf16[128,768]{1,0:T(8,128)(2,1)S(1)} %slice.179), channel_id=1, replica_groups=mesh['ctx'=8,'fsdp'=4] {'fsdp'}, dimensions={0}, use_global_device_ids=true | all-gather | bytes 983040 | tf_op jit(solution)/shard_map/all_gather | solution.py:236
  112.6 21.6 %all_gather.51 = bf16[512,768]{1,0:T(8,128)(2,1)S(1)} all-gather(bf16[128,768]{1,0:T(8,128)(2,1)S(1)} %get-tuple-element.1127), channel_id=1, replica_groups=mesh['ctx'=8,'fsdp'=4] {'fsdp'}, dimensions={0}, use_global_device_ids=true | all-gather | bytes 983040 | tf_op jit(solution)/shard_map/all_gather | solution.py:237
  147.2 181.9 %while.46 = (s32[]{:T(128)}, f32[128,12,64]{0,2,1:T(8,128)S(1)}, f32[12,128]{1,0:T(8,128)}, f32[12,128]{1,0:T(8,128)S(1)}, bf16[512,768]{0,1:T(8,128)(2,1)}, /*i...) while((s32[]{:T(128)}, f32[128,12,64]{0,2,1:T(8,128)S(1)}, ...), condition=%wide.region_24.25_spmd, body=%wide.region_13.24_spmd.sunk | while | flops 711403008 | bytes 26007200 | solution.py:259
  348.1 8.5 conditional.10
  363.2 474.3 %while.47 = (s32[]{:T(128)}, f32[128,12,64]{0,2,1:T(8,128)}, f32[512,768]{0,1:T(8,128)}, f32[512,768]{0,1:T(8,128)}, bf16[512,768]{0,1:T(8,128)(2,1)S(1)}, /*ind...) while((s32[]{:T(128)}, f32[128,12,64]{0,2,1:T(8,128)}, ...), condition=%wide.region_41.42_spmd, body=%wide.region_34.41_spmd.sunk | while | flops 512033280 | bytes 83529712 | solution.py:336
  380.7 28.7 %collective-permute-done.2 = bf16[512,768]{0,1:T(8,128)(2,1)S(1)} collective-permute-done((bf16[512,768]{0,1:T(8,128)(2,1)S(1)}, bf16[512,768]{0,1:T(8,128)(2,1)S(1)}, u32[]{:S(2)}, u32[]{:S(2)}) %collective-permute-start.2) | collective-permute-done | bytes 786464 | tf_op jit(solution)/shard_map/while/body/eval_jaxpr/ppermute | solution.py:19
  409.4 8.4 collective-permute-done.3
  449.9 25.3 %collective-permute-done.2 = bf16[512,768]{0,1:T(8,128)(2,1)S(1)} collective-permute-done((bf16[512,768]{0,1:T(8,128)(2,1)S(1)}, bf16[512,768]{0,1:T(8,128)(2,1)S(1)}, u32[]{:S(2)}, u32[]{:S(2)}) %collective-permute-start.2) | collective-permute-done | bytes 786464 | tf_op jit(solution)/shard_map/while/body/eval_jaxpr/ppermute | solution.py:19
  475.3 8.4 collective-permute-done.3
  501.6 9.6 collective-permute-start.2
  519.1 25.3 %collective-permute-done.2 = bf16[512,768]{0,1:T(8,128)(2,1)S(1)} collective-permute-done((bf16[512,768]{0,1:T(8,128)(2,1)S(1)}, bf16[512,768]{0,1:T(8,128)(2,1)S(1)}, u32[]{:S(2)}, u32[]{:S(2)}) %collective-permute-start.2) | collective-permute-done | bytes 786464 | tf_op jit(solution)/shard_map/while/body/eval_jaxpr/ppermute | solution.py:19
  588.4 25.3 %collective-permute-done.2 = bf16[512,768]{0,1:T(8,128)(2,1)S(1)} collective-permute-done((bf16[512,768]{0,1:T(8,128)(2,1)S(1)}, bf16[512,768]{0,1:T(8,128)(2,1)S(1)}, u32[]{:S(2)}, u32[]{:S(2)}) %collective-permute-start.2) | collective-permute-done | bytes 786464 | tf_op jit(solution)/shard_map/while/body/eval_jaxpr/ppermute | solution.py:19
  657.6 22.0 %collective-permute-done.2 = bf16[512,768]{0,1:T(8,128)(2,1)S(1)} collective-permute-done((bf16[512,768]{0,1:T(8,128)(2,1)S(1)}, bf16[512,768]{0,1:T(8,128)(2,1)S(1)}, u32[]{:S(2)}, u32[]{:S(2)}) %collective-permute-start.2) | collective-permute-done | bytes 786464 | tf_op jit(solution)/shard_map/while/body/eval_jaxpr/ppermute | solution.py:19
  706.5 12.3 collective-permute-start.2
  726.8 22.0 %collective-permute-done.2 = bf16[512,768]{0,1:T(8,128)(2,1)S(1)} collective-permute-done((bf16[512,768]{0,1:T(8,128)(2,1)S(1)}, bf16[512,768]{0,1:T(8,128)(2,1)S(1)}, u32[]{:S(2)}, u32[]{:S(2)}) %collective-permute-start.2) | collective-permute-done | bytes 786464 | tf_op jit(solution)/shard_map/while/body/eval_jaxpr/ppermute | solution.py:19
  748.8 8.4 collective-permute-done.3
  771.5 16.6 %collective-permute-start.2 = (bf16[512,768]{0,1:T(8,128)(2,1)S(1)}, bf16[512,768]{0,1:T(8,128)(2,1)S(1)}, u32[]{:S(2)}, u32[]{:S(2)}) collective-permute-start(bf16[512,768]{0,1:T(8,128)(2,1)S(1)} %get-tuple-element.1467), channel_id=1, source_target_pairs={{28,0},{0,4},{4,8},{8,12},{12,16},{16,20},{20,24},{24,28},{29,1},{... | collective-permute-start | bytes 2359304 | tf_op jit(solution)/shard_map/while/body/eval_jaxpr/ppermute | solution.py:19
  796.0 18.6 %collective-permute-done.2 = bf16[512,768]{0,1:T(8,128)(2,1)S(1)} collective-permute-done((bf16[512,768]{0,1:T(8,128)(2,1)S(1)}, bf16[512,768]{0,1:T(8,128)(2,1)S(1)}, u32[]{:S(2)}, u32[]{:S(2)}) %collective-permute-start.2) | collective-permute-done | bytes 786464 | tf_op jit(solution)/shard_map/while/body/eval_jaxpr/ppermute | solution.py:19
  837.6 20.9 %collective-permute-done.6 = f32[512,768]{0,1:T(8,128)S(1)} collective-permute-done((f32[512,768]{0,1:T(8,128)}, f32[512,768]{0,1:T(8,128)S(1)}, u32[]{:S(2)}, u32[]{:S(2)}) %collective-permute-start.6) | collective-permute-done | bytes 1572896 | tf_op jit(solution)/shard_map/ppermute | solution.py:19
  859.9 20.9 %collective-permute-done.7 = f32[512,768]{0,1:T(8,128)S(1)} collective-permute-done((f32[512,768]{0,1:T(8,128)}, f32[512,768]{0,1:T(8,128)S(1)}, u32[]{:S(2)}, u32[]{:S(2)}) %collective-permute-start.7) | collective-permute-done | bytes 1572896 | tf_op jit(solution)/shard_map/ppermute | solution.py:19
  885.1 82.3 %reduce-scatter.7.cloned.1.call-done = f32[128,768]{0,1:T(8,128)} async-done(((f32[512,768]{0,1:T(8,128)}), f32[128,768]{0,1:T(8,128)}) %reduce-scatter.7.cloned.1.call-update) | async-done | bytes 393232 | tf_op jit(solution)/shard_map/reduce_scatter | solution.py:342
  968.4 36.0 %reduce-scatter.9.cloned.1.call-done = f32[128,768]{0,1:T(8,128)} async-done(((f32[512,768]{0,1:T(8,128)}), f32[128,768]{0,1:T(8,128)}) %reduce-scatter.9.cloned.1.call-update) | async-done | bytes 393232 | tf_op jit(solution)/shard_map/reduce_scatter | solution.py:343
  1023.1 30.8 %reduce-scatter.13.cloned.1.call-done = f32[192,768]{1,0:T(8,128)} async-done(((f32[768,768]{1,0:T(8,128)}), f32[192,768]{1,0:T(8,128)}) %reduce-scatter.13.cloned.1.call-update) | async-done | bytes 589840 | tf_op jit(solution)/shard_map/reduce_scatter | solution.py:362
  1053.9 125.2 %reduce-scatter.11.cloned.1.call-done = f32[192,2304]{1,0:T(8,128)} async-done(((f32[768,2304]{1,0:T(8,128)}), f32[192,2304]{1,0:T(8,128)}) %reduce-scatter.11.cloned.1.call-update) | async-done | bytes 1769488 | tf_op jit(solution)/shard_map/reduce_scatter | solution.py:359
  1179.2 164.1 %reduce-scatter.15.cloned.1.call-done = f32[192,3072]{1,0:T(8,128)} async-done(((f32[768,3072]{1,0:T(8,128)}), f32[192,3072]{1,0:T(8,128)}) %reduce-scatter.15.cloned.1.call-update) | async-done | bytes 2359312 | tf_op jit(solution)/shard_map/reduce_scatter | solution.py:295
  1343.3 164.4 %reduce-scatter.17.cloned.1.call-done = f32[768,768]{1,0:T(8,128)} async-done(((f32[3072,768]{1,0:T(8,128)}), f32[768,768]{1,0:T(8,128)}) %reduce-scatter.17.cloned.1.call-update) | async-done | bytes 2359312 | tf_op jit(solution)/shard_map/reduce_scatter | solution.py:297
  1515.5 19.3 %all-reduce.19 = (f32[768]{0:T(1024)S(1)}, f32[768]{0:T(1024)S(1)}, f32[768]{0:T(1024)S(1)}, f32[768]{0:T(1024)S(1)}, f32[768]{0:T(1024)S(1)}, /*index=5*/f32[76...) all-reduce(f32[768]{0:T(1024)S(1)} %get-tuple-element.1015, ...), channel_id=4, replica_groups=mesh['ctx'=8,'fsdp'=4] {'fsdp'}, use_global_device_ids=true, to_apply=%region_47.48.clone | all-reduce | flops 9216 | bytes 73728
  1535.4 23.3 %all-reduce.17 = (f32[192]{0:T(256)}, f32[192]{0:T(256)}, f32[192]{0:T(256)}, f32[192]{0:T(256)}, f32[192]{0:T(256)}, /*index=5*/f32[192]{0:T(256)}, f32[192]{0:T(256)}, f32[768]{0:T(1024)}, f32[192]{0:T(256)}) all-reduce(f32[192]{0:T(256)S(1)} %dynamic-slice.9, ...), channel_id=1, replica_groups=mesh['ctx'=8,'fsdp'=4] {'ctx'}, use_global_device_ids=true, to_apply=%region_48.49 | all-reduce | flops 2304 | bytes 18432 | tf_op jit(solution)/shard_map/psum | solution.py:365
  1559.6 65.7 %all-reduce.23.cloned.1.call-done = (f32[192,2304]{1,0:T(8,128)}, f32[192,768]{1,0:T(8,128)}, f32[192,3072]{1,0:T(8,128)}, f32[768,768]{1,0:T(8,128)}) async-done(((f32[192,2304]{1,0:T(8,128)}, f32[192,768]{1,0:T(8,128)}, f32[192,3072]{1,0:T(8,128)}, f32[768,768]{1,0:T(8,128)}), (f32[192,2304]{1,0:T(8,128)}, f32[192,768]{1,0:T(8,128)}, f32[192,3072]{1,0:T(8,128)}, ...) | async-done | bytes 7077904 | tf_op jit(solution)/shard_map/psum | solution.py:365
  (725 shorter events, 541.0 us)
Async XLA Ops:
  7.2 75.5 %all-gather.6.cloned.1.call-start = ((), (), s32[]{:S(2)}) async-start(), calls=%async_computation.6 | async-start | bytes 4423680 | tf_op jit(solution)/shard_map/all_gather | solution.py:214
  8.0 321.2 %all-gather.8.cloned.1.call-start = ((), (), s32[]{:S(2)}) async-start(), calls=%async_computation.7 | async-start | bytes 1474560 | tf_op jit(solution)/shard_map/all_gather | solution.py:217
  8.8 323.8 %all-gather.10.cloned.1.call-start = ((), (), s32[]{:S(2)}) async-start(), calls=%async_computation.8 | async-start | bytes 5898240 | tf_op jit(solution)/shard_map/all_gather | solution.py:223
  9.5 327.4 %all-gather.12.cloned.1.call-start = ((), (), s32[]{:S(2)}) async-start(), calls=%async_computation.9 | async-start | bytes 5898240 | tf_op jit(solution)/shard_map/all_gather | solution.py:225
  10.1 957.3 %reduce-scatter.7.cloned.1.call-start = ((), (), s32[]{:S(2)}) async-start(), calls=%async_computation.10 | async-start | bytes 1966080 | tf_op jit(solution)/shard_map/reduce_scatter | solution.py:342
  363.2 59.8 %collective-permute-start.4 = (f32[512,768]{0,1:T(8,128)}, f32[512,768]{0,1:T(8,128)}, u32[]{:S(2)}, u32[]{:S(2)}) collective-permute-start(f32[512,768]{0,1:T(8,128)} %get-tuple-element.1465), channel_id=1, source_target_pairs={{28,0},{0,4},{4,8},{8,12},{12,16},{16,20},{20,24},{24,28},{29,1},{... | collective-permute-start | bytes 4718600 | tf_op jit(solution)/shard_map/while/body/eval_jaxpr/ppermute | solution.py:19
  363.2 62.8 %collective-permute-start.5 = (f32[512,768]{0,1:T(8,128)}, f32[512,768]{0,1:T(8,128)}, u32[]{:S(2)}, u32[]{:S(2)}) collective-permute-start(f32[512,768]{0,1:T(8,128)} %get-tuple-element.1466), channel_id=1, source_target_pairs={{28,0},{0,4},{4,8},{8,12},{12,16},{16,20},{20,24},{24,28},{29,1},{... | collective-permute-start | bytes 4718600 | tf_op jit(solution)/shard_map/while/body/eval_jaxpr/ppermute | solution.py:19
  365.0 44.5 %collective-permute-start.2 = (bf16[512,768]{0,1:T(8,128)(2,1)S(1)}, bf16[512,768]{0,1:T(8,128)(2,1)S(1)}, u32[]{:S(2)}, u32[]{:S(2)}) collective-permute-start(bf16[512,768]{0,1:T(8,128)(2,1)S(1)} %get-tuple-element.1467), channel_id=1, source_target_pairs={{28,0},{0,4},{4,8},{8,12},{12,16},{16,20},{20,24},{24,28},{29,1},{... | collective-permute-start | bytes 2359304 | tf_op jit(solution)/shard_map/while/body/eval_jaxpr/ppermute | solution.py:19
  369.6 48.3 %collective-permute-start.3 = (bf16[512,768]{0,1:T(8,128)(2,1)S(1)}, bf16[512,768]{0,1:T(8,128)(2,1)S(1)}, u32[]{:S(2)}, u32[]{:S(2)}) collective-permute-start(bf16[512,768]{0,1:T(8,128)(2,1)S(1)} %get-tuple-element.1468), channel_id=1, source_target_pairs={{28,0},{0,4},{4,8},{8,12},{12,16},{16,20},{20,24},{24,28},{29,1},{... | collective-permute-start | bytes 2359304 | tf_op jit(solution)/shard_map/while/body/eval_jaxpr/ppermute | solution.py:19
  429.0 63.2 %collective-permute-start.4 = (f32[512,768]{0,1:T(8,128)}, f32[512,768]{0,1:T(8,128)}, u32[]{:S(2)}, u32[]{:S(2)}) collective-permute-start(f32[512,768]{0,1:T(8,128)} %get-tuple-element.1465), channel_id=1, source_target_pairs={{28,0},{0,4},{4,8},{8,12},{12,16},{16,20},{20,24},{24,28},{29,1},{... | collective-permute-start | bytes 4718600 | tf_op jit(solution)/shard_map/while/body/eval_jaxpr/ppermute | solution.py:19
  429.0 66.1 %collective-permute-start.5 = (f32[512,768]{0,1:T(8,128)}, f32[512,768]{0,1:T(8,128)}, u32[]{:S(2)}, u32[]{:S(2)}) collective-permute-start(f32[512,768]{0,1:T(8,128)} %get-tuple-element.1466), channel_id=1, source_target_pairs={{28,0},{0,4},{4,8},{8,12},{12,16},{16,20},{20,24},{24,28},{29,1},{... | collective-permute-start | bytes 4718600 | tf_op jit(solution)/shard_map/while/body/eval_jaxpr/ppermute | solution.py:19
  438.6 45.1 %collective-permute-start.3 = (bf16[512,768]{0,1:T(8,128)(2,1)S(1)}, bf16[512,768]{0,1:T(8,128)(2,1)S(1)}, u32[]{:S(2)}, u32[]{:S(2)}) collective-permute-start(bf16[512,768]{0,1:T(8,128)(2,1)S(1)} %get-tuple-element.1468), channel_id=1, source_target_pairs={{28,0},{0,4},{4,8},{8,12},{12,16},{16,20},{20,24},{24,28},{29,1},{... | collective-permute-start | bytes 2359304 | tf_op jit(solution)/shard_map/while/body/eval_jaxpr/ppermute | solution.py:19
  498.2 63.2 %collective-permute-start.4 = (f32[512,768]{0,1:T(8,128)}, f32[512,768]{0,1:T(8,128)}, u32[]{:S(2)}, u32[]{:S(2)}) collective-permute-start(f32[512,768]{0,1:T(8,128)} %get-tuple-element.1465), channel_id=1, source_target_pairs={{28,0},{0,4},{4,8},{8,12},{12,16},{16,20},{20,24},{24,28},{29,1},{... | collective-permute-start | bytes 4718600 | tf_op jit(solution)/shard_map/while/body/eval_jaxpr/ppermute | solution.py:19
  498.3 66.1 %collective-permute-start.5 = (f32[512,768]{0,1:T(8,128)}, f32[512,768]{0,1:T(8,128)}, u32[]{:S(2)}, u32[]{:S(2)}) collective-permute-start(f32[512,768]{0,1:T(8,128)} %get-tuple-element.1466), channel_id=1, source_target_pairs={{28,0},{0,4},{4,8},{8,12},{12,16},{16,20},{20,24},{24,28},{29,1},{... | collective-permute-start | bytes 4718600 | tf_op jit(solution)/shard_map/while/body/eval_jaxpr/ppermute | solution.py:19
  501.6 42.9 %collective-permute-start.2 = (bf16[512,768]{0,1:T(8,128)(2,1)S(1)}, bf16[512,768]{0,1:T(8,128)(2,1)S(1)}, u32[]{:S(2)}, u32[]{:S(2)}) collective-permute-start(bf16[512,768]{0,1:T(8,128)(2,1)S(1)} %get-tuple-element.1467), channel_id=1, source_target_pairs={{28,0},{0,4},{4,8},{8,12},{12,16},{16,20},{20,24},{24,28},{29,1},{... | collective-permute-start | bytes 2359304 | tf_op jit(solution)/shard_map/while/body/eval_jaxpr/ppermute | solution.py:19
  567.4 59.8 %collective-permute-start.4 = (f32[512,768]{0,1:T(8,128)}, f32[512,768]{0,1:T(8,128)}, u32[]{:S(2)}, u32[]{:S(2)}) collective-permute-start(f32[512,768]{0,1:T(8,128)} %get-tuple-element.1465), channel_id=1, source_target_pairs={{28,0},{0,4},{4,8},{8,12},{12,16},{16,20},{20,24},{24,28},{29,1},{... | collective-permute-start | bytes 4718600 | tf_op jit(solution)/shard_map/while/body/eval_jaxpr/ppermute | solution.py:19
  567.5 62.7 %collective-permute-start.5 = (f32[512,768]{0,1:T(8,128)}, f32[512,768]{0,1:T(8,128)}, u32[]{:S(2)}, u32[]{:S(2)}) collective-permute-start(f32[512,768]{0,1:T(8,128)} %get-tuple-element.1466), channel_id=1, source_target_pairs={{28,0},{0,4},{4,8},{8,12},{12,16},{16,20},{20,24},{24,28},{29,1},{... | collective-permute-start | bytes 4718600 | tf_op jit(solution)/shard_map/while/body/eval_jaxpr/ppermute | solution.py:19
  569.9 43.8 %collective-permute-start.2 = (bf16[512,768]{0,1:T(8,128)(2,1)S(1)}, bf16[512,768]{0,1:T(8,128)(2,1)S(1)}, u32[]{:S(2)}, u32[]{:S(2)}) collective-permute-start(bf16[512,768]{0,1:T(8,128)(2,1)S(1)} %get-tuple-element.1467), channel_id=1, source_target_pairs={{28,0},{0,4},{4,8},{8,12},{12,16},{16,20},{20,24},{24,28},{29,1},{... | collective-permute-start | bytes 2359304 | tf_op jit(solution)/shard_map/while/body/eval_jaxpr/ppermute | solution.py:19
  577.0 45.1 %collective-permute-start.3 = (bf16[512,768]{0,1:T(8,128)(2,1)S(1)}, bf16[512,768]{0,1:T(8,128)(2,1)S(1)}, u32[]{:S(2)}, u32[]{:S(2)}) collective-permute-start(bf16[512,768]{0,1:T(8,128)(2,1)S(1)} %get-tuple-element.1468), channel_id=1, source_target_pairs={{28,0},{0,4},{4,8},{8,12},{12,16},{16,20},{20,24},{24,28},{29,1},{... | collective-permute-start | bytes 2359304 | tf_op jit(solution)/shard_map/while/body/eval_jaxpr/ppermute | solution.py:19
  633.2 63.2 %collective-permute-start.4 = (f32[512,768]{0,1:T(8,128)}, f32[512,768]{0,1:T(8,128)}, u32[]{:S(2)}, u32[]{:S(2)}) collective-permute-start(f32[512,768]{0,1:T(8,128)} %get-tuple-element.1465), channel_id=1, source_target_pairs={{28,0},{0,4},{4,8},{8,12},{12,16},{16,20},{20,24},{24,28},{29,1},{... | collective-permute-start | bytes 4718600 | tf_op jit(solution)/shard_map/while/body/eval_jaxpr/ppermute | solution.py:19
  633.3 66.1 %collective-permute-start.5 = (f32[512,768]{0,1:T(8,128)}, f32[512,768]{0,1:T(8,128)}, u32[]{:S(2)}, u32[]{:S(2)}) collective-permute-start(f32[512,768]{0,1:T(8,128)} %get-tuple-element.1466), channel_id=1, source_target_pairs={{28,0},{0,4},{4,8},{8,12},{12,16},{16,20},{20,24},{24,28},{29,1},{... | collective-permute-start | bytes 4718600 | tf_op jit(solution)/shard_map/while/body/eval_jaxpr/ppermute | solution.py:19
  702.5 59.8 %collective-permute-start.4 = (f32[512,768]{0,1:T(8,128)}, f32[512,768]{0,1:T(8,128)}, u32[]{:S(2)}, u32[]{:S(2)}) collective-permute-start(f32[512,768]{0,1:T(8,128)} %get-tuple-element.1465), channel_id=1, source_target_pairs={{28,0},{0,4},{4,8},{8,12},{12,16},{16,20},{20,24},{24,28},{29,1},{... | collective-permute-start | bytes 4718600 | tf_op jit(solution)/shard_map/while/body/eval_jaxpr/ppermute | solution.py:19
  702.5 62.7 %collective-permute-start.5 = (f32[512,768]{0,1:T(8,128)}, f32[512,768]{0,1:T(8,128)}, u32[]{:S(2)}, u32[]{:S(2)}) collective-permute-start(f32[512,768]{0,1:T(8,128)} %get-tuple-element.1466), channel_id=1, source_target_pairs={{28,0},{0,4},{4,8},{8,12},{12,16},{16,20},{20,24},{24,28},{29,1},{... | collective-permute-start | bytes 4718600 | tf_op jit(solution)/shard_map/while/body/eval_jaxpr/ppermute | solution.py:19
  768.3 63.2 %collective-permute-start.4 = (f32[512,768]{0,1:T(8,128)}, f32[512,768]{0,1:T(8,128)}, u32[]{:S(2)}, u32[]{:S(2)}) collective-permute-start(f32[512,768]{0,1:T(8,128)} %get-tuple-element.1465), channel_id=1, source_target_pairs={{28,0},{0,4},{4,8},{8,12},{12,16},{16,20},{20,24},{24,28},{29,1},{... | collective-permute-start | bytes 4718600 | tf_op jit(solution)/shard_map/while/body/eval_jaxpr/ppermute | solution.py:19
  769.0 65.5 %collective-permute-start.5 = (f32[512,768]{0,1:T(8,128)}, f32[512,768]{0,1:T(8,128)}, u32[]{:S(2)}, u32[]{:S(2)}) collective-permute-start(f32[512,768]{0,1:T(8,128)} %get-tuple-element.1466), channel_id=1, source_target_pairs={{28,0},{0,4},{4,8},{8,12},{12,16},{16,20},{20,24},{24,28},{29,1},{... | collective-permute-start | bytes 4718600 | tf_op jit(solution)/shard_map/while/body/eval_jaxpr/ppermute | solution.py:19
  771.5 43.1 %collective-permute-start.2 = (bf16[512,768]{0,1:T(8,128)(2,1)S(1)}, bf16[512,768]{0,1:T(8,128)(2,1)S(1)}, u32[]{:S(2)}, u32[]{:S(2)}) collective-permute-start(bf16[512,768]{0,1:T(8,128)(2,1)S(1)} %get-tuple-element.1467), channel_id=1, source_target_pairs={{28,0},{0,4},{4,8},{8,12},{12,16},{16,20},{20,24},{24,28},{29,1},{... | collective-permute-start | bytes 2359304 | tf_op jit(solution)/shard_map/while/body/eval_jaxpr/ppermute | solution.py:19
  859.7 144.7 %reduce-scatter.9.cloned.1.call-start = ((), (), s32[]{:S(2)}) async-start(), calls=%async_computation.11 | async-start | bytes 1966080 | tf_op jit(solution)/shard_map/reduce_scatter | solution.py:343
  882.0 172.0 %reduce-scatter.13.cloned.1.call-start = ((), (), s32[]{:S(2)}) async-start(), calls=%async_computation.13 | async-start | bytes 2949120 | tf_op jit(solution)/shard_map/reduce_scatter | solution.py:362
  883.9 295.2 %reduce-scatter.11.cloned.1.call-start = ((), (), s32[]{:S(2)}) async-start(), calls=%async_computation.12 | async-start | bytes 8847360 | tf_op jit(solution)/shard_map/reduce_scatter | solution.py:359
  1010.1 333.2 %reduce-scatter.15.cloned.1.call-start = ((), (), s32[]{:S(2)}) async-start(), calls=%async_computation.14 | async-start | bytes 11796480 | tf_op jit(solution)/shard_map/reduce_scatter | solution.py:295
  1016.5 491.2 %reduce-scatter.17.cloned.1.call-start = ((), (), s32[]{:S(2)}) async-start(), calls=%async_computation.15 | async-start | bytes 11796480 | tf_op jit(solution)/shard_map/reduce_scatter | solution.py:297
  1023.1 602.3 %all-reduce.23.cloned.1.call-start = ((), (), s32[]{:S(2)}) async-start(), calls=%async_computation.16 | async-start | bytes 14155776 | tf_op jit(solution)/shard_map/psum | solution.py:365
  (172 other events, 2355.6 us)
Sparse Core Ops, SparseCore 0:
  9.6 73.1 all-gather.5
  84.3 42.3 all-gather.7
  128.2 89.0 all-gather.9
  218.8 87.7 all-gather.11
  859.9 107.5 reduce-scatter.6
  970.2 34.2 reduce-scatter.8
  1007.3 46.5 reduce-scatter.12
  1056.2 122.8 reduce-scatter.10
  1181.5 161.6 reduce-scatter.14
  1345.5 162.1 reduce-scatter.16
  1511.3 113.9 all-reduce.22
where the time goes:
time: 1650 us; the launch traced here: 1640 us
  waiting for transfers between devices  1060 us (64%)
  starting transfers between devices  147 us (9%)
  blocking collectives  126 us (8%)
  local copies, waits for them, and re-layouts  92.7 us (6%)
  other arithmetic  90.5 us (5%)
  matrix products  64.5 us (4%)
  loops' own time  38.4 us (2%)
  between operations  19.7 us (1%)
    ppermute x44, waiting for transfers between devices, passed_along(): return lax.ppermute(block, axis, route)  365 us
    reduce_scatter x1, waiting for transfers between devices, shards(): lax.psum_scatter(out_weight_grad, 'fsdp', scatter_dimension=0, tiled=True)  164 us
    reduce_scatter x1, waiting for transfers between devices, shards(): lax.psum_scatter(fc_weight_grad, 'fsdp', scatter_dimension=0, tiled=True)  164 us
    ppermute x44, starting transfers between devices, passed_along(): return lax.ppermute(block, axis, route)  147 us
    reduce_scatter x1, waiting for transfers between devices, shards(): lax.psum_scatter(qkv_weight_grad, 'fsdp', scatter_dimension=0, tiled=True)  125 us
    reduce_scatter x1, waiting for transfers between devices, shards(): lax.psum_scatter(key_grads[0], 'fsdp', scatter_dimension=0, tiled=True)  82.3 us
    psum x1, waiting for transfers between devices, shards(): lax.psum((attn_shares[0], attn_shares[1], attn_shares[2], attn_shares[3],...  65.7 us
    unnamed x2, blocking collectives  41.2 us
  transfers between devices with their start and end apart: 55, of which 38 were waited for; matrix products, arithmetic and copies ran while one was open for 11% of the time, Pallas kernels for 0%

commit v1 on v0

--- a/solution.py
+++ b/solution.py
@@ -1,6 +1,10 @@
+import functools
+
 import jax
 import jax.numpy as jnp
 from jax import lax
+from jax.experimental import pallas as pl
+from jax.experimental.pallas import tpu as pltpu
 from jax.sharding import PartitionSpec as P
 
 HEADS = 12
@@ -399,6 +403,346 @@
     )
 
 
+def head_cols(head, offset=0):
+    return slice(offset + head * HEAD, offset + (head + 1) * HEAD)
+
+
+def tile_keep(block, key_block, query_block):
+    key_row = lax.broadcasted_iota(jnp.int32, (block, block), 0)
+    query_col = lax.broadcasted_iota(jnp.int32, (block, block), 1)
+    return key_row <= query_col + jnp.where(key_block == query_block, 0, block)
+
+
+def forward_kernel(
+    heads, block, ids_ref, own_ref, q_ref, kv_ref, out_ref, lse_ref, max_ref, sum_ref, acc_ref
+):
+    span = heads * HEAD
+    max_ref[...] = jnp.full_like(max_ref, NEG_FILL)
+    sum_ref[...] = jnp.zeros_like(sum_ref)
+    acc_ref[...] = jnp.zeros_like(acc_ref)
+
+    def step(index, carry):
+        first = pl.multiple_of(index * block, block)
+        key_block = ids_ref[index]
+        for part in range(2):
+            cols = slice(part * block, (part + 1) * block)
+            query_block = own_ref[part]
+
+            @pl.when(key_block <= query_block)
+            def _():
+                keep = tile_keep(block, key_block, query_block)
+                for head in range(heads):
+                    k = kv_ref[pl.ds(first, block), head_cols(head)]
+                    v = kv_ref[pl.ds(first, block), head_cols(head, span)]
+                    q = q_ref[cols, head_cols(head)]
+                    scores = jnp.where(keep, transposed_product(k, q), NEG_FILL)
+                    old_max = max_ref[head : head + 1, cols]
+                    new_max = jnp.maximum(old_max, jnp.max(scores, axis=0, keepdims=True))
+                    weights = jnp.exp(scores - new_max)
+                    factor = jnp.exp(old_max - new_max)
+                    max_ref[head : head + 1, cols] = new_max
+                    sum_ref[head : head + 1, cols] = sum_ref[
+                        head : head + 1, cols
+                    ] * factor + jnp.sum(weights, axis=0, keepdims=True)
+                    acc_ref[head_cols(head), cols] = acc_ref[
+                        head_cols(head), cols
+                    ] * factor + rows_product(v, weights.astype(jnp.bfloat16))
+
+        return carry
+
+    lax.fori_loop(0, kv_ref.shape[0] // block, step, 0)
+    for head in range(heads):
+        total = sum_ref[head : head + 1, :]
+        out_ref[head_cols(head), :] = (acc_ref[head_cols(head), :] / total).astype(out_ref.dtype)
+        lse_ref[head : head + 1, :] = max_ref[head : head + 1, :] + jnp.log(total)
+
+
+def backward_kernel(
+    heads, block, ids_ref, own_ref, q_ref, kv_ref, do_ref, lse_ref, delta_ref, dq_ref, dkv_ref, acc_ref
+):
+    span = heads * HEAD
+    dq_ref[...] = jnp.zeros_like(dq_ref)
+
+    def step(index, carry):
+        first = pl.multiple_of(index * block, block)
+        key_block = ids_ref[index]
+        acc_ref[...] = jnp.zeros_like(acc_ref)
+        for part in range(2):
+            cols = slice(part * block, (part + 1) * block)
+            query_block = own_ref[part]
+
+            @pl.when(key_block <= query_block)
+            def _():
+                keep = tile_keep(block, key_block, query_block)
+                key_parts = []
+                value_parts = []
+                for head in range(heads):
+                    k = kv_ref[pl.ds(first, block), head_cols(head)]
+                    v = kv_ref[pl.ds(first, block), head_cols(head, span)]
+                    q = q_ref[cols, head_cols(head)]
+                    do = do_ref[cols, head_cols(head)]
+                    scores = jnp.where(keep, transposed_product(k, q), NEG_FILL)
+                    probs = jnp.exp(scores - lse_ref[head : head + 1, cols])
+                    value_parts.append(
+                        jnp.dot(
+                            probs.astype(jnp.bfloat16), do, preferred_element_type=jnp.float32
+                        )
+                    )
+                    grad_probs = transposed_product(v, do)
+                    grad_scores = (
+                        probs * (grad_probs - delta_ref[head : head + 1, cols])
+                    ).astype(jnp.bfloat16)
+                    key_parts.append(
+                        jnp.dot(grad_scores, q, preferred_element_type=jnp.float32)
+                    )
+                    dq_ref[head_cols(head), cols] += rows_product(k, grad_scores)
+                acc_ref[...] += jnp.concatenate(key_parts + value_parts, axis=1)
+
+        dkv_ref[pl.ds(first, block), :] = acc_ref[...].astype(dkv_ref.dtype)
+        return carry
+
+    lax.fori_loop(0, kv_ref.shape[0] // block, step, 0)
+
+
+SMEM = pltpu.SMEM
+VMEM = pltpu.VMEM
+
+
+def attention_forward(heads, block, ids, own, q, kv):
+    group_rows, span = q.shape
+    return pl.pallas_call(
+        functools.partial(forward_kernel, heads, block),
+        out_shape=(
+            jax.ShapeDtypeStruct((span, group_rows), jnp.bfloat16),
+            jax.ShapeDtypeStruct((heads, group_rows), jnp.float32),
+        ),
+        in_specs=[pl.BlockSpec(memory_space=SMEM)] * 2 + [pl.BlockSpec(memory_space=VMEM)] * 2,
+        out_specs=(pl.BlockSpec(memory_space=VMEM),) * 2,
+        scratch_shapes=[
+            VMEM((heads, group_rows), jnp.float32),
+            VMEM((heads, group_rows), jnp.float32),
+            VMEM((span, group_rows), jnp.float32),
+        ],
+        cost_estimate=pl.CostEstimate(
+            flops=2 * group_rows * kv.shape[0] * span,
+            bytes_accessed=2 * kv.size,
+            transcendentals=group_rows * kv.shape[0] * heads // 2,
+        ),
+        name="attention_forward",
+    )(ids, own, q, kv)
+
+
+def attention_backward(heads, block, ids, own, q, kv, do, lse, delta):
+    group_rows, span = q.shape
+    return pl.pallas_call(
+        functools.partial(backward_kernel, heads, block),
+        out_shape=(
+            jax.ShapeDtypeStruct((span, group_rows), jnp.float32),
+            jax.ShapeDtypeStruct(kv.shape, jnp.bfloat16),
+        ),
+        in_specs=[pl.BlockSpec(memory_space=SMEM)] * 2 + [pl.BlockSpec(memory_space=VMEM)] * 5,
+        out_specs=(pl.BlockSpec(memory_space=VMEM),) * 2,
+        scratch_shapes=[VMEM((block, 2 * span), jnp.float32)],
+        cost_estimate=pl.CostEstimate(
+            flops=5 * group_rows * kv.shape[0] * span,
+            bytes_accessed=4 * kv.size,
+            transcendentals=group_rows * kv.shape[0] * heads // 2,
+        ),
+        name="attention_backward",
+    )(ids, own, q, kv, do, lse, delta)
+
+
+def head_shards(
+    block_input,
+    positions,
+    norm1_gain,
+    norm1_bias,
+    qkv_weight,
+    query_bias,
+    value_bias,
+    proj_weight,
+    proj_bias,
+    norm2_gain,
+    norm2_bias,
+    fc_weight,
+    fc_bias,
+    out_weight,
+    out_bias,
+    cotangent,
+):
+    rows, width = block_input.shape
+    ctx_size = lax.axis_size("ctx")
+    members = lax.axis_size("fsdp")
+    ctx_index = lax.axis_index("ctx")
+    member = lax.axis_index("fsdp")
+    group_rows = rows * members
+    block = group_rows // 2
+    span = width // members
+    heads = HEADS // members
+    hidden = fc_weight.shape[1] // members
+    piece = span // ctx_size
+    f32, b16 = jnp.float32, jnp.bfloat16
+
+    def gathered(value, axis=0):
+        return lax.all_gather(value, "fsdp", axis=axis, tiled=True)
+
+    def scattered(value):
+        return lax.psum_scatter(value, "fsdp", scatter_dimension=0, tiled=True)
+
+    def exchanged(value):
+        return lax.all_to_all(value, "fsdp", 0, 0, tiled=True)
+
+    def own_rows(value):
+        return lax.dynamic_slice_in_dim(value, member * rows, rows)
+
+    input_all = gathered(block_input)
+    qkv_cols = exchanged(
+        qkv_weight.reshape(span, 3, members, span).transpose(2, 0, 1, 3).reshape(members, span, 3 * span)
+    ).reshape(width, 3 * span)
+    vectors = gathered(
+        jnp.stack([norm1_gain, norm1_bias, proj_bias, norm2_gain, norm2_bias, out_bias]), axis=1
+    )
+    gain_one, shift_one, pbias, gain_two, shift_two, obias = (vectors[i] for i in range(6))
+    proj_full = gathered(proj_weight)
+    fc_cols = exchanged(fc_weight.reshape(span, members, hidden).transpose(1, 0, 2)).reshape(
+        width, hidden
+    )
+    cotangent_all = gathered(cotangent)
+
+    ids = positions.reshape(2 * ctx_size, block)[:, 0] // block
+    own_ids = lax.dynamic_slice_in_dim(ids, 2 * ctx_index, 2)
+
+    residual = input_all.astype(f32)
+    norm1 = layer_norm(residual, gain_one, shift_one)[0].astype(b16)
+    qkv = jnp.dot(norm1, qkv_cols, preferred_element_type=f32)
+    query = (qkv[:, :span] + query_bias.astype(f32)).astype(b16)
+    keys = qkv[:, span : 2 * span].astype(b16)
+    values = (qkv[:, 2 * span :] + value_bias.astype(f32)).astype(b16)
+    query = query * jnp.asarray(HEAD**-0.5, b16)
+    all_kv = lax.all_gather(jnp.concatenate([keys, values], axis=1), "ctx", axis=0, tiled=True)
+    attn_t, lse = attention_forward(heads, block, ids, own_ids, query, all_kv)
+    attn_all_t = gathered(attn_t)
+    middle_all = residual + rows_product(attn_all_t, proj_full) + pbias.astype(f32)
+    norm2 = layer_norm(middle_all, gain_two, shift_two)[0].astype(b16)
+    pre_act = jnp.dot(norm2, fc_cols, preferred_element_type=f32) + fc_bias.astype(f32)
+    act = gelu_forward(pre_act).astype(b16)
+    grad_act = transposed_product(cotangent_all, out_weight)
+    grad_pre = grad_act * gelu_slope(pre_act)
+    fc_bias_grad = jnp.sum(grad_pre, axis=0)
+    grad_pre_half = grad_pre.astype(b16)
+    grad_norm2 = scattered(transposed_product(grad_pre_half, fc_cols).astype(b16)).astype(f32)
+    middle = own_rows(middle_all)
+    _, normed2, inv_std2 = layer_norm(middle, gain_two, shift_two)
+    grad_out = cotangent.astype(f32)
+    grad_middle = grad_out + norm_backward(grad_norm2, gain_two, normed2, inv_std2)
+    grad_middle_all = gathered(grad_middle.astype(b16))
+
+    mlp_out = scattered(jnp.dot(act, out_weight, preferred_element_type=f32).astype(b16))
+    block_output = middle + mlp_out.astype(f32) + obias.astype(f32)
+
+    grad_attn = transposed_product(grad_middle_all, proj_weight).astype(b16)
+    delta = jnp.sum(
+        (grad_attn.T.astype(f32) * attn_t.astype(f32)).reshape(heads, HEAD, group_rows), axis=1
+    )
+    grad_query_t, grad_kv = attention_backward(
+        heads, block, ids, own_ids, query, all_kv, grad_attn, lse, delta
+    )
+    own_kv = lax.psum_scatter(grad_kv, "ctx", scatter_dimension=0, tiled=True)
+
+    out_weight_grad = rows_product(act, cotangent_all).astype(b16)
+    fc_weight_grad = rows_product(norm2, grad_pre_half).astype(b16)
+    proj_weight_grad = jnp.dot(attn_t, grad_middle_all, preferred_element_type=f32).astype(b16)
+    shares = jnp.concatenate(
+        [
+            out_weight_grad.reshape(ctx_size, -1, width),
+            proj_weight_grad.reshape(ctx_size, piece, width),
+            fc_weight_grad.reshape(members, ctx_size, piece, hidden)
+            .transpose(1, 0, 2, 3)
+            .reshape(ctx_size, members * piece, hidden),
+        ],
+        axis=1,
+    )
+    shares = lax.psum_scatter(shares, "ctx", scatter_dimension=0, tiled=True)[0]
+    kept = shares.shape[0] - members * piece
+    shares = jnp.concatenate([shares[:kept], exchanged(shares[kept:])], axis=0)
+    shares = lax.all_gather(shares, "ctx", axis=0, tiled=False)
+    out_rows = out_weight.shape[0] // ctx_size
+    out_weight_grad = shares[:, :out_rows].reshape(out_weight.shape).astype(f32)
+    proj_weight_grad = shares[:, out_rows:kept].reshape(proj_weight.shape).astype(f32)
+    fc_weight_grad = (
+        shares[:, kept:]
+        .reshape(ctx_size, members, piece, hidden)
+        .transpose(0, 2, 1, 3)
+        .reshape(fc_weight.shape)
+        .astype(f32)
+    )
+
+    grad_query = grad_query_t.T * HEAD**-0.5
+    grad_qkv = jnp.concatenate([grad_query.astype(b16), own_kv], axis=1)
+    grad_norm1 = scattered(transposed_product(grad_qkv, qkv_cols).astype(b16)).astype(f32)
+    qkv_share = rows_product(norm1, grad_qkv).astype(b16)
+    qkv_share = (
+        qkv_share.reshape(members, ctx_size, piece, 3 * span)
+        .transpose(1, 0, 2, 3)
+        .reshape(ctx_size, members * piece, 3 * span)
+    )
+    qkv_share = lax.psum_scatter(qkv_share, "ctx", scatter_dimension=0, tiled=True)[0]
+    qkv_share = lax.all_gather(exchanged(qkv_share), "ctx", axis=0, tiled=False)
+    qkv_weight_grad = (
+        qkv_share.reshape(ctx_size, members, piece, 3, span)
+        .transpose(0, 2, 3, 1, 4)
+        .reshape(qkv_weight.shape)
+        .astype(f32)
+    )
+    _, normed1, inv_std1 = layer_norm(block_input.astype(f32), gain_one, shift_one)
+    input_grad = grad_middle + norm_backward(grad_norm1, gain_one, normed1, inv_std1)
+
+    split_sums = jnp.concatenate(
+        [
+            jnp.sum(grad_query, axis=0),
+            jnp.sum(own_kv[:, span:].astype(f32), axis=0),
+            fc_bias_grad,
+        ]
+    )
+    row_sums = jnp.stack(
+        [
+            jnp.sum(grad_norm1 * normed1, axis=0),
+            jnp.sum(grad_norm1, axis=0),
+            jnp.sum(grad_middle, axis=0),
+            jnp.sum(grad_norm2 * normed2, axis=0),
+            jnp.sum(grad_norm2, axis=0),
+            jnp.sum(grad_out, axis=0),
+        ]
+    ).reshape(6, members, span)
+    own_slot = (jnp.arange(members) == member)[:, None]
+    sums = jnp.concatenate(
+        [
+            row_sums.transpose(1, 0, 2).reshape(members, 6 * span),
+            jnp.where(own_slot, split_sums[None], 0.0),
+        ],
+        axis=1,
+    )
+    sums = lax.dynamic_index_in_dim(lax.psum(sums, ("ctx", "fsdp")), member, keepdims=False)
+    parts = sums[: 8 * span].reshape(8, span)
+    return (
+        block_output,
+        input_grad,
+        parts[0],
+        parts[1],
+        qkv_weight_grad,
+        parts[6],
+        parts[7],
+        proj_weight_grad,
+        parts[2],
+        parts[3],
+        parts[4],
+        fc_weight_grad,
+        sums[8 * span :],
+        out_weight_grad,
+        parts[5],
+    )
+
+
 def solution(mesh):
     in_specs = (
         P(("ctx", "fsdp"), None),
@@ -435,4 +779,7 @@
         P("fsdp", None),
         P("fsdp"),
     )
-    return jax.shard_map(shards, mesh=mesh, in_specs=in_specs, out_specs=out_specs, check_vma=False)
+    members = mesh.shape["fsdp"]
+    by_heads = HEADS % members == 0 and (HEADS // members * HEAD) % mesh.shape["ctx"] == 0
+    body = head_shards if by_heads else shards
+    return jax.shard_map(body, mesh=mesh, in_specs=in_specs, out_specs=out_specs, check_vma=False)

time: 1650 us -> 490 us (0.30)
  waiting for transfers between devices: 1060 us -> 156 us
  starting transfers between devices: 147 us -> 20.6 us
  other arithmetic: 90.5 us -> 17.3 us
  local copies, waits for them, and re-layouts: 92.7 us -> 40.3 us
  blocking collectives: 126 us -> 176 us
  matrix products: 64.5 us -> 22.4 us
  Pallas kernels: 0 us -> 41.8 us
  loops' own time: 38.4 us -> 0 us
    reduce_scatter x6, waiting for transfers between devices: 603 us -> 144 us  [the longest x3 41.3 us: scattered(): return lax.psum_scatter(value, 'fsdp', scatter_dimension=0, tiled=True)]
    ppermute x44 -> x0, waiting for transfers between devices: 365 us -> none  [passed_along(): return lax.ppermute(block, axis, route)]
    ppermute x44 -> x0, starting transfers between devices: 147 us -> none  [passed_along(): return lax.ppermute(block, axis, route)]
    all_gather x3 -> x6, blocking collectives: 61.3 us -> 136 us  [the longest x5 124 us: gathered(): return lax.all_gather(value, 'fsdp', axis=axis, tiled=True)]
    psum x1 -> x0, waiting for transfers between devices: 65.7 us -> none  [shards(): lax.psum((attn_shares[0], attn_shares[1], attn_shares[2], attn_shares[3],...]
    add x29 -> x2, other arithmetic: 56.5 us -> 2.48 us  [the longest x1 1.86 us: head_shards(): grad_middle + norm_backward(grad_norm1, gain_one, normed1, inv_std1)]
    pallas_call x0 -> x2, Pallas kernels: none -> 41.8 us  [the longest x1 22.9 us: attention_backward(): pl.pallas_call(functools.partial(backward_kernel, heads, block), out_shap...]
    unnamed x2 -> x0, blocking collectives: 41.2 us -> none
  transfers between devices with their start and end apart: 55 -> 13, of which waited for: 38 -> 7; matrix products, arithmetic and copies ran while one was open for 11% -> 10% of each run, Pallas kernels for 0% -> 4%
where the time goes in v1:
time: 490 us; the launch traced here: 488 us
  blocking collectives  176 us (36%)
  waiting for transfers between devices  156 us (32%)
  Pallas kernels  41.8 us (9%)
  local copies, waits for them, and re-layouts  40.3 us (8%)
  matrix products  22.4 us (5%)
  starting transfers between devices  20.6 us (4%)
  other arithmetic  17.3 us (4%)
  between operations  14.5 us (3%)
    all_gather x5, blocking collectives, gathered(): return lax.all_gather(value, 'fsdp', axis=axis, tiled=True)  124 us
    reduce_scatter x3, waiting for transfers between devices, scattered(): return lax.psum_scatter(value, 'fsdp', scatter_dimension=0, tiled=True)  41.3 us
    reduce_scatter x1, waiting for transfers between devices, head_shards(): shares = lax.psum_scatter(shares, 'ctx', scatter_dimension=0, tiled=True)[0]  40.2 us
    psum x1, blocking collectives, head_shards(): lax.psum(sums, ('ctx', 'fsdp'))  39.4 us
    reduce_scatter x1, waiting for transfers between devices, head_shards(): own_kv = lax.psum_scatter(grad_kv, 'ctx', scatter_dimension=0, tiled=True)  36.9 us
    reduce_scatter x1, waiting for transfers between devices, head_shards(): lax.psum_scatter(qkv_share, 'ctx', scatter_dimension=0, tiled=True)[0]  25.4 us
    pallas_call x1, Pallas kernels, attention_backward(): pl.pallas_call(functools.partial(backward_kernel, heads, block), out_shap...  22.9 us
    all_to_all x4, starting transfers between devices, exchanged(): return lax.all_to_all(value, 'fsdp', 0, 0, tiled=True)  20.1 us
  transfers between devices with their start and end apart: 13, of which 7 were waited for; matrix products, arithmetic and copies ran while one was open for 10% of the time, Pallas kernels for 4%

profile of v1, /device:TPU:0, one launch (start us, length us, event | category | flops | bytes accessed | tf_op | source)
XLA Modules:
  0.0 488.5 jit_solution(13796683953178933028)
XLA Ops:
  7.2 3.0 reshape.205
  12.6 6.5 %all-to-all-start = ((bf16[4,192,576]{2,1,0:T(8,128)(2,1)}), bf16[4,192,576]{2,1,0:T(8,128)(2,1)S(1)}, u32[]{:S(2)}, u32[]{:S(2)}) async-start(bf16[4,192,576]{2,1,0:T(8,128)(2,1)} %copy.85), calls=%async_computation | async-start | bytes 1966080 | tf_op jit(solution)/shard_map/all_to_all | solution.py:593
  19.3 29.7 %all-gather.1 = bf16[4,192,6]{1,2,0:T(8,128)(2,1)S(1)} all-gather(bf16[1,192,6]{1,2,0:T(8,128)(2,1)S(1)} %bitcast.94), channel_id=1, replica_groups=mesh['ctx'=8,'fsdp'=4] {'fsdp'}, dimensions={0}, use_global_device_ids=true | all-gather | bytes 11520 | tf_op jit(solution)/shard_map/all_gather | solution.py:587
  49.7 17.4 %all_gather.33 = bf16[512,768]{1,0:T(8,128)(2,1)S(1)} all-gather(bf16[128,768]{1,0:T(8,128)(2,1)S(1)} %copy-done.2), channel_id=1, replica_groups=mesh['ctx'=8,'fsdp'=4] {'fsdp'}, dimensions={0}, use_global_device_ids=true | all-gather | bytes 983040 | tf_op jit(solution)/shard_map/all_gather | solution.py:587
  71.2 2.7 reshape.208
  75.1 4.4 all-to-all-start.1
  80.4 41.9 %all_gather.38 = bf16[512,768]{1,0:T(8,128)(2,1)} all-gather(bf16[128,768]{1,0:T(8,128)(2,1)S(1)} %copy-done.13), channel_id=1, replica_groups=mesh['ctx'=8,'fsdp'=4] {'fsdp'}, dimensions={0}, use_global_device_ids=true | all-gather | bytes 983040 | tf_op jit(solution)/shard_map/all_gather | solution.py:587
  123.2 18.9 %attention_forward.1 = (bf16[192,512]{1,0:T(8,128)(2,1)}, f32[3,512]{1,0:T(4,128)}) custom-call(s32[16]{0:T(128)} %copy-done.41, s32[2]{0:T(128)} %dynamic_slice.10.own_ref, bf16[512,192]{1,0:T(8,128)(2,1)} %fusion.37.q_ref, bf16[4096,384]{1,0:T(8,128)(2,1)} %all-gather.6.cloned.1.call-done.kv_ref), custom_call_target="tpu_custom_call" | custom-call | flops 805306368 | bytes 3145728 | tf_op jit(solution)/shard_map/attention_forward/pallas_call | solution.py:513
  142.1 17.6 %all_gather.36 = bf16[768,512]{1,0:T(8,128)(2,1)} all-gather(bf16[192,512]{1,0:T(8,128)(2,1)} %get-tuple-element.19), channel_id=1, replica_groups=mesh['ctx'=8,'fsdp'=4] {'fsdp'}, dimensions={0}, use_global_device_ids=true | all-gather | bytes 983040 | tf_op jit(solution)/shard_map/all_gather | solution.py:587
  159.7 2.4 fusion.53
  163.1 2.3 convolution_add_fusion
  168.3 3.0 convolution_convert_fusion.3
  171.5 3.4 convolution_convert_fusion.4
  177.2 17.6 %reduce-scatter.9.cloned.1.call-done = bf16[128,768]{1,0:T(8,128)(2,1)} async-done(((bf16[512,768]{1,0:T(8,128)(2,1)}), bf16[128,768]{1,0:T(8,128)(2,1)}) %reduce-scatter.9.cloned.1.call-update) | async-done | bytes 196624 | tf_op jit(solution)/shard_map/reduce_scatter | solution.py:590
  195.9 23.7 %reduce-scatter.7.cloned.1.call-done = bf16[128,768]{1,0:T(8,128)(2,1)} async-done(((bf16[512,768]{1,0:T(8,128)(2,1)}), bf16[128,768]{1,0:T(8,128)(2,1)}) %reduce-scatter.7.cloned.1.call-update) | async-done | bytes 196624 | tf_op jit(solution)/shard_map/reduce_scatter | solution.py:590
  219.6 2.6 fusion.49
  222.3 17.9 %all_gather.39 = bf16[512,768]{1,0:T(8,128)(2,1)S(1)} all-gather(bf16[128,768]{1,0:T(8,128)(2,1)S(1)} %convert_element_type.157), channel_id=1, replica_groups=mesh['ctx'=8,'fsdp'=4] {'fsdp'}, dimensions={0}, use_global_device_ids=true | all-gather | bytes 983040 | tf_op jit(solution)/shard_map/all_gather | solution.py:587
  243.4 22.9 %attention_backward.1 = (f32[192,512]{1,0:T(8,128)}, bf16[4096,384]{1,0:T(8,128)(2,1)}) custom-call(s32[16]{0:T(128)} %copy-done.41, s32[2]{0:T(128)} %dynamic_slice.10.own_ref, bf16[512,192]{1,0:T(8,128)(2,1)} %fusion.37.q_ref, bf16[4096,384]{1,0:T(8,128)(2,1)} %all-gather.6.cloned.1.call-done.kv_ref, bf16[512,192]{1,0:T(8,128)(2,1)} %get-tuple-element.58.do_ref, ...), custom_call_target="tpu_custom_call" | custom-call | flops 2013265920 | bytes 6291456 | tf_op jit(solution)/shard_map/attention_backward/pallas_call | solution.py:537
  267.0 2.1 convolution_convert_fusion
  275.1 36.9 %reduce-scatter.11.cloned.1.call-done = bf16[512,384]{1,0:T(8,128)(2,1)} async-done(((bf16[4096,384]{1,0:T(8,128)(2,1)}), bf16[512,384]{1,0:T(8,128)(2,1)}) %reduce-scatter.11.cloned.1.call-update) | async-done | bytes 393232 | tf_op jit(solution)/shard_map/reduce_scatter | solution.py:650
  312.0 2.1 convolution_convert_fusion.2
  318.2 40.2 %reduce-scatter.17.cloned.1.call-done = bf16[1,216,768]{2,1,0:T(8,128)(2,1)} async-done(((bf16[8,216,768]{2,1,0:T(8,128)(2,1)}), bf16[1,216,768]{2,1,0:T(8,128)(2,1)}) %reduce-scatter.17.cloned.1.call-update) | async-done | bytes 331792 | tf_op jit(solution)/shard_map/reduce_scatter | solution.py:665
  360.0 4.6 all-to-all-start.3
  365.5 5.3 %all-to-all-done.3 = bf16[4,24,768]{2,1,0:T(8,128)(2,1)S(1)} async-done(((bf16[4,24,768]{2,1,0:T(8,128)(2,1)}), bf16[4,24,768]{2,1,0:T(8,128)(2,1)S(1)}, u32[]{:S(2)}, u32[]{:S(2)}) %all-to-all-start.3) | async-done | bytes 147488 | tf_op jit(solution)/shard_map/all_to_all | solution.py:593
  372.5 25.4 %reduce-scatter.15.cloned.1.call-done = bf16[1,96,576]{2,1,0:T(8,128)(2,1)} async-done(((bf16[8,96,576]{2,1,0:T(8,128)(2,1)}), bf16[1,96,576]{2,1,0:T(8,128)(2,1)}) %reduce-scatter.15.cloned.1.call-update) | async-done | bytes 110608 | tf_op jit(solution)/shard_map/reduce_scatter | solution.py:689
  398.0 4.6 all-to-all-start.2
  402.6 5.8 %all-to-all-done.2 = bf16[4,24,576]{2,1,0:T(8,128)(2,1)S(1)} async-done(((bf16[4,24,576]{2,1,0:T(8,128)(2,1)}), bf16[4,24,576]{2,1,0:T(8,128)(2,1)S(1)}, u32[]{:S(2)}, u32[]{:S(2)}) %all-to-all-start.2) | async-done | bytes 110624 | tf_op jit(solution)/shard_map/all_to_all | solution.py:593
  408.5 12.0 %all_gather.41 = bf16[8,96,576]{2,1,0:T(8,128)(2,1)} all-gather(bf16[1,96,576]{2,1,0:T(8,128)(2,1)S(1)} %bitcast.90), channel_id=1, replica_groups=mesh['ctx'=8,'fsdp'=4] {'ctx'}, dimensions={0}, use_global_device_ids=true | all-gather | bytes 995328 | tf_op jit(solution)/shard_map/all_gather | solution.py:690
  420.4 3.2 reshape.228
  423.6 2.9 copy.96
  426.5 3.7 reshape.224
  431.8 39.4 %psum.7 = f32[4,2304]{1,0:T(4,128)S(1)} all-reduce(f32[4,2304]{1,0:T(4,128)S(1)} %pad_maximum_fusion.6), channel_id=1, replica_groups=mesh['ctx'=8,'fsdp'=4] {'ctx','fsdp'}, use_global_device_ids=true, to_apply=%region_26.27 | all-reduce | flops 9216 | bytes 73728 | tf_op jit(solution)/shard_map/psum | solution.py:725
  (203 shorter events, 47.9 us)
Async XLA Ops:
  7.2 158.2 %copy-start = (bf16[768,768]{1,0:T(8,128)(2,1)S(1)}, bf16[768,768]{1,0:T(8,128)(2,1)}, u32[]{:S(2)}) copy-start(bf16[768,768]{1,0:T(8,128)(2,1)} %param.29) | copy-start | bytes 3538948
  11.3 8.0 %copy-start.38 = (bf16[192]{0:T(256)(128)(2,1)S(1)}, bf16[192]{0:T(256)(128)(2,1)}, u32[]{:S(2)}) copy-start(bf16[192]{0:T(256)(128)(2,1)} %param.26) | copy-start | bytes 1156
  11.3 8.0 %copy-start.39 = (bf16[192]{0:T(256)(128)(2,1)S(1)}, bf16[192]{0:T(256)(128)(2,1)}, u32[]{:S(2)}) copy-start(bf16[192]{0:T(256)(128)(2,1)} %param.30) | copy-start | bytes 1156
  12.6 37.0 %copy-start.2 = (bf16[128,768]{1,0:T(8,128)(2,1)S(1)}, bf16[128,768]{1,0:T(8,128)(2,1)}, u32[]{:S(2)}) copy-start(bf16[128,768]{1,0:T(8,128)(2,1)} %param.16) | copy-start | bytes 589828
  12.6 55.0 %all-to-all-start = ((bf16[4,192,576]{2,1,0:T(8,128)(2,1)}), bf16[4,192,576]{2,1,0:T(8,128)(2,1)S(1)}, u32[]{:S(2)}, u32[]{:S(2)}) async-start(bf16[4,192,576]{2,1,0:T(8,128)(2,1)} %copy.85), calls=%async_computation | async-start | bytes 1966080 | tf_op jit(solution)/shard_map/all_to_all | solution.py:593
  19.1 104.1 %all-gather.6.cloned.1.call-start = ((), (), s32[]{:S(2)}) async-start(), calls=%async_computation.10 | async-start | bytes 3538944 | tf_op jit(solution)/shard_map/all_gather | solution.py:622
  49.7 19.4 %copy-start.26 = (f32[768]{0:T(1024)}, f32[768]{0:T(1024)S(1)}, u32[]{:S(2)}) copy-start(f32[768]{0:T(1024)S(1)} %get-tuple-element.35) | copy-start | bytes 9220
  70.5 89.2 %all-gather.8.cloned.1.call-start = ((), (), s32[]{:S(2)}) async-start(), calls=%async_computation.11 | async-start | bytes 1474560 | tf_op jit(solution)/shard_map/all_gather | solution.py:587
  75.1 88.0 %all-to-all-start.1 = ((bf16[4,192,768]{2,1,0:T(8,128)(2,1)}), bf16[4,192,768]{2,1,0:T(8,128)(2,1)}, u32[]{:S(2)}, u32[]{:S(2)}) async-start(bf16[4,192,768]{2,1,0:T(8,128)(2,1)} %copy.89), calls=%async_computation.1 | async-start | bytes 2359296 | tf_op jit(solution)/shard_map/all_to_all | solution.py:593
  79.5 115.2 %reduce-scatter.9.cloned.1.call-start = ((), (), s32[]{:S(2)}) async-start(), calls=%async_computation.13 | async-start | bytes 983040 | tf_op jit(solution)/shard_map/reduce_scatter | solution.py:590
  79.8 43.4 %copy-start.41 = (s32[16]{0:T(128)}, s32[16]{0:T(128)S(1)}, u32[]{:S(2)}) copy-start(s32[16]{0:T(128)S(1)} %and_select_fusion.ids_ref) | copy-start | bytes 196
  171.3 48.4 %reduce-scatter.7.cloned.1.call-start = ((), (), s32[]{:S(2)}) async-start(), calls=%async_computation.12 | async-start | bytes 983040 | tf_op jit(solution)/shard_map/reduce_scatter | solution.py:590
  174.9 44.8 %copy-start.14 = (bf16[128,768]{1,0:T(8,128)(2,1)S(1)}, bf16[128,768]{1,0:T(8,128)(2,1)}, u32[]{:S(2)}) copy-start(bf16[128,768]{1,0:T(8,128)(2,1)} %param.31) | copy-start | bytes 589828
  174.9 44.8 %copy-start.19 = (f32[768]{0:T(1024)S(1)}, f32[768]{0:T(1024)}, u32[]{:S(2)}) copy-start(f32[768]{0:T(1024)} %get-tuple-element.31) | copy-start | bytes 9220
  174.9 137.1 %reduce-scatter.11.cloned.1.call-start = ((), (), s32[]{:S(2)}) async-start(), calls=%async_computation.14 | async-start | bytes 3538944 | tf_op jit(solution)/shard_map/reduce_scatter | solution.py:650
  219.6 20.6 %copy-start.6 = (f32[192,512]{0,1:T(8,128)S(1)}, f32[192,512]{0,1:T(8,128)}, u32[]{:S(2)}) copy-start(f32[192,512]{0,1:T(8,128)} %copy.91) | copy-start | bytes 1179652
  219.6 20.6 %copy-start.8 = (bf16[192,768]{1,0:T(8,128)(2,1)S(1)}, bf16[192,768]{1,0:T(8,128)(2,1)}, u32[]{:S(2)}) copy-start(bf16[192,768]{1,0:T(8,128)(2,1)} %param.23) | copy-start | bytes 884740
  222.3 19.2 %copy-start.4 = (f32[128,768]{1,0:T(8,128)}, f32[128,768]{1,0:T(8,128)S(1)}, u32[]{:S(2)}) copy-start(f32[128,768]{1,0:T(8,128)S(1)} %get-tuple-element.38) | copy-start | bytes 1179652
  266.3 92.1 %reduce-scatter.17.cloned.1.call-start = ((), (), s32[]{:S(2)}) async-start(), calls=%async_computation.17 | async-start | bytes 2985984 | tf_op jit(solution)/shard_map/reduce_scatter | solution.py:665
  273.8 38.3 %copy-start.22 = (f32[512]{0:T(512)S(1)}, f32[512]{0:T(512)}, u32[]{:S(2)}) copy-start(f32[512]{0:T(512)} %copy-done.21) | copy-start | bytes 6148
  273.8 38.3 %copy-start.27 = (f32[768]{0:T(1024)S(1)}, f32[768]{0:T(1024)}, u32[]{:S(2)}) copy-start(f32[768]{0:T(1024)} %copy-done.26) | copy-start | bytes 9220
  273.8 38.3 %copy-start.31 = (f32[512]{0:T(512)S(1)}, f32[512]{0:T(512)}, u32[]{:S(2)}) copy-start(f32[512]{0:T(512)} %copy-done.30) | copy-start | bytes 6148
  273.8 124.2 %reduce-scatter.15.cloned.1.call-start = ((), (), s32[]{:S(2)}) async-start(), calls=%async_computation.16 | async-start | bytes 1105920 | tf_op jit(solution)/shard_map/reduce_scatter | solution.py:689
  315.9 114.4 %reduce-scatter.13.cloned.1.call-start = ((), (), s32[]{:S(2)}) async-start(), calls=%async_computation.15 | async-start | bytes 983040 | tf_op jit(solution)/shard_map/reduce_scatter | solution.py:590
  318.1 53.5 %copy-start.3 = (bf16[128,768]{1,0:T(8,128)(2,1)S(1)}, bf16[128,768]{1,0:T(8,128)(2,1)}, u32[]{:S(2)}) copy-start(bf16[128,768]{1,0:T(8,128)(2,1)} %param.16) | copy-start | bytes 589828
  318.1 54.0 %copy-start.18 = (f32[768]{0:T(1024)S(1)}, f32[768]{0:T(1024)}, u32[]{:S(2)}) copy-start(f32[768]{0:T(1024)} %get-tuple-element.37) | copy-start | bytes 9220
  318.1 54.1 %copy-start.17 = (f32[768]{0:T(1024)S(1)}, f32[768]{0:T(1024)}, u32[]{:S(2)}) copy-start(f32[768]{0:T(1024)} %get-tuple-element.46) | copy-start | bytes 9220
  318.1 54.3 %copy-start.25 = (f32[768]{0:T(1024)S(1)}, f32[768]{0:T(1024)}, u32[]{:S(2)}) copy-start(f32[768]{0:T(1024)} %get-tuple-element.59) | copy-start | bytes 9220
  360.0 10.8 %all-to-all-start.3 = ((bf16[4,24,768]{2,1,0:T(8,128)(2,1)}), bf16[4,24,768]{2,1,0:T(8,128)(2,1)S(1)}, u32[]{:S(2)}, u32[]{:S(2)}) async-start(bf16[4,24,768]{2,1,0:T(8,128)(2,1)} %bitcast.28), calls=%async_computation.9 | async-start | bytes 294912 | tf_op jit(solution)/shard_map/all_to_all | solution.py:593
  364.6 109.8 %all-gather.10.cloned.1.call-start = ((), (), s32[]{:S(2)}) async-start(), calls=%async_computation.18 | async-start | bytes 2985984 | tf_op jit(solution)/shard_map/all_gather | solution.py:668
  398.0 10.5 %all-to-all-start.2 = ((bf16[4,24,576]{2,1,0:T(8,128)(2,1)}), bf16[4,24,576]{2,1,0:T(8,128)(2,1)S(1)}, u32[]{:S(2)}, u32[]{:S(2)}) async-start(bf16[4,24,576]{2,1,0:T(8,128)(2,1)} %bitcast.92), calls=%async_computation.7 | async-start | bytes 245760 | tf_op jit(solution)/shard_map/all_to_all | solution.py:593
  426.5 46.0 %copy-start.5 = (f32[128,768]{1,0:T(8,128)S(1)}, f32[128,768]{1,0:T(8,128)}, u32[]{:S(2)}) copy-start(f32[128,768]{1,0:T(8,128)} %copy-done.4) | copy-start | bytes 1179652
  (26 other events, 81.2 us)
Sparse Core Ops, SparseCore 0:
  70.6 32.1 all-gather.5
  104.4 32.6 all-gather.7
  171.4 23.3 reduce-scatter.8
  196.9 22.6 reduce-scatter.6
  266.5 45.5 reduce-scatter.10
  315.4 42.9 reduce-scatter.16
  362.2 35.7 reduce-scatter.14
  400.8 23.1 reduce-scatter.12
  426.5 29.9 all-gather.9

commit v2 on v1

--- a/solution.py
+++ b/solution.py
@@ -587,7 +587,11 @@
         return lax.all_gather(value, "fsdp", axis=axis, tiled=True)
 
     def scattered(value):
-        return lax.psum_scatter(value, "fsdp", scatter_dimension=0, tiled=True)
+        shares_in = lax.all_to_all(value.reshape(members, rows, width), "fsdp", 0, 0, tiled=True)
+        return jnp.sum(shares_in.astype(f32), axis=0)
+
+    def group_sum(value):
+        return lax.psum_scatter(value, "ctx", scatter_dimension=0, tiled=True)[0]
 
     def exchanged(value):
         return lax.all_to_all(value, "fsdp", 0, 0, tiled=True)
@@ -595,19 +599,24 @@
     def own_rows(value):
         return lax.dynamic_slice_in_dim(value, member * rows, rows)
 
-    input_all = gathered(block_input)
+    vectors = jnp.concatenate(
+        [norm1_gain, norm1_bias, proj_bias, norm2_gain, norm2_bias, out_bias]
+    )
+    vectors = jnp.pad(vectors, (0, 16 * width - vectors.size)).reshape(16, width)
+    combined = lax.all_gather(
+        jnp.concatenate([block_input, cotangent, vectors], axis=0), "fsdp", axis=0
+    )
+    input_all = combined[:, :rows].reshape(group_rows, width)
+    cotangent_all = combined[:, rows : 2 * rows].reshape(group_rows, width)
+    vectors = combined[:, 2 * rows :].reshape(members, 16 * width)[:, : 6 * span]
+    vectors = vectors.reshape(members, 6, span).transpose(1, 0, 2).reshape(6, width)
     qkv_cols = exchanged(
         qkv_weight.reshape(span, 3, members, span).transpose(2, 0, 1, 3).reshape(members, span, 3 * span)
     ).reshape(width, 3 * span)
-    vectors = gathered(
-        jnp.stack([norm1_gain, norm1_bias, proj_bias, norm2_gain, norm2_bias, out_bias]), axis=1
-    )
     gain_one, shift_one, pbias, gain_two, shift_two, obias = (vectors[i] for i in range(6))
-    proj_full = gathered(proj_weight)
     fc_cols = exchanged(fc_weight.reshape(span, members, hidden).transpose(1, 0, 2)).reshape(
         width, hidden
     )
-    cotangent_all = gathered(cotangent)
 
     ids = positions.reshape(2 * ctx_size, block)[:, 0] // block
     own_ids = lax.dynamic_slice_in_dim(ids, 2 * ctx_index, 2)
@@ -620,6 +629,8 @@
     values = (qkv[:, 2 * span :] + value_bias.astype(f32)).astype(b16)
     query = query * jnp.asarray(HEAD**-0.5, b16)
     all_kv = lax.all_gather(jnp.concatenate([keys, values], axis=1), "ctx", axis=0, tiled=True)
+    all_kv, proj_late = lax.optimization_barrier((all_kv, proj_weight))
+    proj_full = gathered(proj_late)
     attn_t, lse = attention_forward(heads, block, ids, own_ids, query, all_kv)
     attn_all_t = gathered(attn_t)
     middle_all = residual + rows_product(attn_all_t, proj_full) + pbias.astype(f32)
@@ -637,18 +648,7 @@
     grad_middle = grad_out + norm_backward(grad_norm2, gain_two, normed2, inv_std2)
     grad_middle_all = gathered(grad_middle.astype(b16))
 
-    mlp_out = scattered(jnp.dot(act, out_weight, preferred_element_type=f32).astype(b16))
-    block_output = middle + mlp_out.astype(f32) + obias.astype(f32)
-
     grad_attn = transposed_product(grad_middle_all, proj_weight).astype(b16)
-    delta = jnp.sum(
-        (grad_attn.T.astype(f32) * attn_t.astype(f32)).reshape(heads, HEAD, group_rows), axis=1
-    )
-    grad_query_t, grad_kv = attention_backward(
-        heads, block, ids, own_ids, query, all_kv, grad_attn, lse, delta
-    )
-    own_kv = lax.psum_scatter(grad_kv, "ctx", scatter_dimension=0, tiled=True)
-
     out_weight_grad = rows_product(act, cotangent_all).astype(b16)
     fc_weight_grad = rows_product(norm2, grad_pre_half).astype(b16)
     proj_weight_grad = jnp.dot(attn_t, grad_middle_all, preferred_element_type=f32).astype(b16)
@@ -662,7 +662,18 @@
         ],
         axis=1,
     )
-    shares = lax.psum_scatter(shares, "ctx", scatter_dimension=0, tiled=True)[0]
+    mlp_share = jnp.dot(act, out_weight, preferred_element_type=f32).astype(b16)
+    grad_attn, shares, mlp_share = lax.optimization_barrier((grad_attn, shares, mlp_share))
+    delta = jnp.sum(
+        (grad_attn.T.astype(f32) * attn_t.astype(f32)).reshape(heads, HEAD, group_rows), axis=1
+    )
+    grad_query_t, grad_kv = attention_backward(
+        heads, block, ids, own_ids, query, all_kv, grad_attn, lse, delta
+    )
+    block_output = middle + scattered(mlp_share).astype(f32) + obias.astype(f32)
+    own_kv = group_sum(grad_kv.reshape(ctx_size, group_rows, 2 * span))
+
+    shares = group_sum(shares)
     kept = shares.shape[0] - members * piece
     shares = jnp.concatenate([shares[:kept], exchanged(shares[kept:])], axis=0)
     shares = lax.all_gather(shares, "ctx", axis=0, tiled=False)
@@ -681,49 +692,53 @@
     grad_qkv = jnp.concatenate([grad_query.astype(b16), own_kv], axis=1)
     grad_norm1 = scattered(transposed_product(grad_qkv, qkv_cols).astype(b16)).astype(f32)
     qkv_share = rows_product(norm1, grad_qkv).astype(b16)
-    qkv_share = (
-        qkv_share.reshape(members, ctx_size, piece, 3 * span)
-        .transpose(1, 0, 2, 3)
-        .reshape(ctx_size, members * piece, 3 * span)
-    )
-    qkv_share = lax.psum_scatter(qkv_share, "ctx", scatter_dimension=0, tiled=True)[0]
+    _, normed1, inv_std1 = layer_norm(block_input.astype(f32), gain_one, shift_one)
+    input_grad = grad_middle + norm_backward(grad_norm1, gain_one, normed1, inv_std1)
+
+    def pieces(vector):
+        return vector.reshape(members, ctx_size, -1)
+
+    def slotted(vector):
+        own_slot = (jnp.arange(members) == member)[:, None, None]
+        return jnp.where(own_slot, vector.reshape(1, ctx_size, -1), 0.0)
+
+    riders = jnp.concatenate(
+        [
+            pieces(jnp.sum(grad_norm1 * normed1, axis=0)),
+            pieces(jnp.sum(grad_norm1, axis=0)),
+            pieces(jnp.sum(grad_middle, axis=0)),
+            pieces(jnp.sum(grad_norm2 * normed2, axis=0)),
+            pieces(jnp.sum(grad_norm2, axis=0)),
+            pieces(jnp.sum(grad_out, axis=0)),
+            slotted(jnp.sum(grad_query, axis=0)),
+            slotted(jnp.sum(own_kv[:, span:].astype(f32), axis=0)),
+            slotted(fc_bias_grad),
+        ],
+        axis=2,
+    )
+    used = riders.shape[2]
+    riders = jnp.pad(riders, ((0, 0), (0, 0), (0, 3 * span - used))).astype(b16)
+    qkv_share = jnp.concatenate(
+        [
+            qkv_share.reshape(members, ctx_size, piece, 3 * span),
+            jnp.broadcast_to(riders[:, :, None], (members, ctx_size, 8, 3 * span)),
+        ],
+        axis=2,
+    )
+    deep = piece + 8
+    qkv_share = qkv_share.transpose(1, 0, 2, 3).reshape(ctx_size, members * deep, 3 * span)
+    qkv_share = group_sum(qkv_share)
     qkv_share = lax.all_gather(exchanged(qkv_share), "ctx", axis=0, tiled=False)
+    qkv_share = qkv_share.reshape(ctx_size, members, deep, 3 * span)
     qkv_weight_grad = (
-        qkv_share.reshape(ctx_size, members, piece, 3, span)
+        qkv_share[:, :, :piece]
+        .reshape(ctx_size, members, piece, 3, span)
         .transpose(0, 2, 3, 1, 4)
         .reshape(qkv_weight.shape)
         .astype(f32)
     )
-    _, normed1, inv_std1 = layer_norm(block_input.astype(f32), gain_one, shift_one)
-    input_grad = grad_middle + norm_backward(grad_norm1, gain_one, normed1, inv_std1)
-
-    split_sums = jnp.concatenate(
-        [
-            jnp.sum(grad_query, axis=0),
-            jnp.sum(own_kv[:, span:].astype(f32), axis=0),
-            fc_bias_grad,
-        ]
-    )
-    row_sums = jnp.stack(
-        [
-            jnp.sum(grad_norm1 * normed1, axis=0),
-            jnp.sum(grad_norm1, axis=0),
-            jnp.sum(grad_middle, axis=0),
-            jnp.sum(grad_norm2 * normed2, axis=0),
-            jnp.sum(grad_norm2, axis=0),
-            jnp.sum(grad_out, axis=0),
-        ]
-    ).reshape(6, members, span)
-    own_slot = (jnp.arange(members) == member)[:, None]
-    sums = jnp.concatenate(
-        [
-            row_sums.transpose(1, 0, 2).reshape(members, 6 * span),
-            jnp.where(own_slot, split_sums[None], 0.0),
-        ],
-        axis=1,
-    )
-    sums = lax.dynamic_index_in_dim(lax.psum(sums, ("ctx", "fsdp")), member, keepdims=False)
-    parts = sums[: 8 * span].reshape(8, span)
+    sums = jnp.sum(qkv_share[:, :, piece, :used].astype(f32), axis=1)
+    parts = [sums[:, i * piece : (i + 1) * piece].reshape(span) for i in range(8)]
     return (
         block_output,
         input_grad,
@@ -737,7 +752,7 @@
         parts[3],
         parts[4],
         fc_weight_grad,
-        sums[8 * span :],
+        sums[:, 8 * piece :].reshape(hidden),
         out_weight_grad,
         parts[5],
     )

time: 490 us -> 496 us (1.012)
  blocking collectives: 176 us -> 64.1 us
  waiting for transfers between devices: 156 us -> 231 us
  local copies, waits for them, and re-layouts: 40.3 us -> 57.4 us
  other arithmetic: 17.3 us -> 30.2 us
  starting transfers between devices: 20.6 us -> 28.5 us
    all_gather x5 -> x2, blocking collectives: 124 us -> 52.6 us  [gathered(): return lax.all_gather(value, 'fsdp', axis=axis, tiled=True)]
    all_gather x0 -> x2, waiting for transfers between devices: none -> 66 us  [the longest x1 51.5 us: head_shards(): lax.all_gather(jnp.concatenate([block_input, cotangent, vectors], axis=0)...]
    reduce_scatter x6 -> x3, waiting for transfers between devices: 144 us -> 87.9 us  [group_sum(): return lax.psum_scatter(value, 'ctx', scatter_dimension=0, tiled=True)[0]]
    all_to_all x0 -> x3, waiting for transfers between devices: none -> 40.2 us  [scattered(): lax.all_to_all(value.reshape(members, rows, width), 'fsdp', 0, 0, tiled=T...]
    psum x1 -> x0, blocking collectives: 39.4 us -> none  [head_shards(): lax.psum(sums, ('ctx', 'fsdp'))]
    all_gather x1, waiting for transfers between devices: 0.01 us -> 31.4 us  [head_shards(): lax.all_gather(jnp.concatenate([keys, values], axis=1), 'ctx', axis=0, ti...]
    all_to_all x0 -> x3, starting transfers between devices: none -> 12.6 us  [scattered(): lax.all_to_all(value.reshape(members, rows, width), 'fsdp', 0, 0, tiled=T...]
    all_gather x1 -> x0, blocking collectives: 12 us -> none  [head_shards(): qkv_share = lax.all_gather(exchanged(qkv_share), 'ctx', axis=0, tiled=False)]
  transfers between devices with their start and end apart: 13 -> 14, of which waited for: 7 -> 10; matrix products, arithmetic and copies ran while one was open for 10% -> 12% of each run, Pallas kernels for 4% -> 4%
where the time goes in v2:
time: 496 us; the launch traced here: 494 us
  waiting for transfers between devices  231 us (47%)
  blocking collectives  64.1 us (13%)
  local copies, waits for them, and re-layouts  57.4 us (12%)
  Pallas kernels  41.8 us (8%)
  other arithmetic  30.2 us (6%)
  starting transfers between devices  28.5 us (6%)
  matrix products  25.6 us (5%)
  between operations  14.7 us (3%)
    reduce_scatter x3, waiting for transfers between devices, group_sum(): return lax.psum_scatter(value, 'ctx', scatter_dimension=0, tiled=True)[0]  87.9 us
    all_gather x2, blocking collectives, gathered(): return lax.all_gather(value, 'fsdp', axis=axis, tiled=True)  52.6 us
    all_gather x1, waiting for transfers between devices, head_shards(): lax.all_gather(jnp.concatenate([block_input, cotangent, vectors], axis=0)...  51.5 us
    all_to_all x3, waiting for transfers between devices, scattered(): lax.all_to_all(value.reshape(members, rows, width), 'fsdp', 0, 0, tiled=T...  40.2 us
    all_gather x1, waiting for transfers between devices, head_shards(): lax.all_gather(jnp.concatenate([keys, values], axis=1), 'ctx', axis=0, ti...  31.4 us
    pallas_call x1, Pallas kernels, attention_backward(): pl.pallas_call(functools.partial(backward_kernel, heads, block), out_shap...  23 us
    pallas_call x1, Pallas kernels, attention_forward(): pl.pallas_call(functools.partial(forward_kernel, heads, block), out_shape...  18.9 us
    all_to_all x3, starting transfers between devices, exchanged(): return lax.all_to_all(value, 'fsdp', 0, 0, tiled=True)  15.6 us
  transfers between devices with their start and end apart: 14, of which 10 were waited for; matrix products, arithmetic and copies ran while one was open for 12% of the time, Pallas kernels for 4%

profile of v2, /device:TPU:0, one launch (start us, length us, event | category | flops | bytes accessed | tf_op | source)
XLA Modules:
  0.0 493.7 jit_solution(12081065100778440990)
XLA Ops:
  7.3 4.2 concatenate.25
  16.9 6.3 %all-to-all-start = ((bf16[4,192,576]{2,1,0:T(8,128)(2,1)}), bf16[4,192,576]{2,1,0:T(8,128)(2,1)}, u32[]{:S(2)}, u32[]{:S(2)}) async-start(bf16[4,192,576]{2,1,0:T(8,128)(2,1)} %copy.101), calls=%async_computation | async-start | bytes 1966080 | tf_op jit(solution)/shard_map/all_to_all | solution.py:597
  23.2 51.5 %all-gather.14.cloned.1.call-done = bf16[1088,768]{1,0:T(8,128)(2,1)} async-done(((bf16[272,768]{1,0:T(8,128)(2,1)}), bf16[1088,768]{1,0:T(8,128)(2,1)}) %all-gather.14.cloned.1.call-update) | async-done | bytes 1671184 | tf_op jit(solution)/shard_map/all_gather | solution.py:606
  87.3 31.4 %all-gather.8.cloned.1.call-done.kv_ref = bf16[4096,384]{1,0:T(8,128)(2,1)} async-done(((bf16[512,384]{1,0:T(8,128)(2,1)}), bf16[4096,384]{1,0:T(8,128)(2,1)}) %all-gather.8.cloned.1.call-update) | async-done | bytes 3145744 | tf_op jit(solution)/shard_map/all_gather | solution.py:631
  118.8 3.5 reshape.360
  124.7 4.7 all-to-all-start.1
  133.6 18.9 %attention_forward.1 = (bf16[192,512]{1,0:T(8,128)(2,1)}, f32[3,512]{1,0:T(4,128)}) custom-call(s32[16]{0:T(128)} %copy-done.20, s32[2]{0:T(128)} %dynamic_slice.6.own_ref, bf16[512,192]{1,0:T(8,128)(2,1)} %fusion.32.q_ref, bf16[4096,384]{1,0:T(8,128)(2,1)} %all-gather.8.cloned.1.call-done.kv_ref), custom_call_target="tpu_custom_call" | custom-call | flops 805306368 | bytes 3145728 | tf_op jit(solution)/shard_map/attention_forward/pallas_call | solution.py:513
  154.3 34.8 %all_gather.33 = bf16[768,512]{1,0:T(8,128)(2,1)} all-gather(bf16[192,512]{1,0:T(8,128)(2,1)} %get-tuple-element.25), channel_id=1, replica_groups=mesh['ctx'=8,'fsdp'=4] {'fsdp'}, dimensions={0}, use_global_device_ids=true | all-gather | bytes 983040 | tf_op jit(solution)/shard_map/all_gather | solution.py:587
  189.1 2.6 fusion.50
  193.2 2.7 convolution_add_fusion
  197.5 3.1 convolution_convert_fusion.4
  202.8 4.3 all-to-all-start.2
  207.1 2.5 copy.107
  214.8 11.9 %all-to-all-done.2 = bf16[4,128,768]{2,1,0:T(8,128)(2,1)} async-done(((bf16[4,128,768]{2,1,0:T(8,128)(2,1)}), bf16[4,128,768]{2,1,0:T(8,128)(2,1)}, u32[]{:S(2)}, u32[]{:S(2)}) %all-to-all-start.2) | async-done | bytes 786464 | tf_op jit(solution)/shard_map/all_to_all | solution.py:590
  230.5 17.8 %all_gather.35 = bf16[512,768]{1,0:T(8,128)(2,1)S(1)} all-gather(bf16[128,768]{1,0:T(8,128)(2,1)S(1)} %convert_element_type.236), channel_id=1, replica_groups=mesh['ctx'=8,'fsdp'=4] {'fsdp'}, dimensions={0}, use_global_device_ids=true | all-gather | bytes 983040 | tf_op jit(solution)/shard_map/all_gather | solution.py:587
  253.7 23.0 %attention_backward.1 = (f32[192,512]{1,0:T(8,128)}, bf16[4096,384]{1,0:T(8,128)(2,1)}) custom-call(s32[16]{0:T(128)} %copy-done.20, s32[2]{0:T(128)} %dynamic_slice.6.own_ref, bf16[512,192]{1,0:T(8,128)(2,1)} %fusion.32.q_ref, bf16[4096,384]{1,0:T(8,128)(2,1)} %all-gather.8.cloned.1.call-done.kv_ref, bf16[512,192]{1,0:T(8,128)(2,1)} %convolution_convert_fusion.7.do_ref, ...), custom_call_target="tpu_custom_call" | custom-call | flops 2013265920 | bytes 6291456 | tf_op jit(solution)/shard_map/attention_backward/pallas_call | solution.py:537
  278.2 43.8 %reduce-scatter.4.cloned.1.call-done = bf16[1,512,384]{2,1,0:T(8,128)(2,1)} async-done(((bf16[8,512,384]{2,1,0:T(8,128)(2,1)}), bf16[1,512,384]{2,1,0:T(8,128)(2,1)}) %reduce-scatter.4.cloned.1.call-update) | async-done | bytes 393232 | tf_op jit(solution)/shard_map/reduce_scatter | solution.py:594
  322.0 3.0 convolution_convert_fusion.5
  325.1 4.8 all-to-all-start.4
  334.3 3.1 convolution_convert_fusion.2
  339.1 10.7 %all-to-all-done.4 = bf16[4,128,768]{2,1,0:T(8,128)(2,1)S(1)} async-done(((bf16[4,128,768]{2,1,0:T(8,128)(2,1)}), bf16[4,128,768]{2,1,0:T(8,128)(2,1)S(1)}, u32[]{:S(2)}, u32[]{:S(2)}) %all-to-all-start.4) | async-done | bytes 786464 | tf_op jit(solution)/shard_map/all_to_all | solution.py:590
  352.1 16.3 %reduce-scatter.8.cloned.1.call-done = bf16[1,216,768]{2,1,0:T(8,128)(2,1)} async-done(((bf16[8,216,768]{2,1,0:T(8,128)(2,1)}), bf16[1,216,768]{2,1,0:T(8,128)(2,1)}) %reduce-scatter.8.cloned.1.call-update) | async-done | bytes 331792 | tf_op jit(solution)/shard_map/reduce_scatter | solution.py:594
  370.0 4.6 all-to-all-start.6
  375.5 5.3 %all-to-all-done.6 = bf16[4,24,768]{2,1,0:T(8,128)(2,1)S(1)} async-done(((bf16[4,24,768]{2,1,0:T(8,128)(2,1)}), bf16[4,24,768]{2,1,0:T(8,128)(2,1)S(1)}, u32[]{:S(2)}, u32[]{:S(2)}) %all-to-all-start.6) | async-done | bytes 147488 | tf_op jit(solution)/shard_map/all_to_all | solution.py:597
  381.6 27.7 %reduce-scatter.6.cloned.1.call-done = bf16[1,128,576]{2,1,0:T(8,128)(2,1)} async-done(((bf16[8,128,576]{2,1,0:T(8,128)(2,1)}), bf16[1,128,576]{2,1,0:T(8,128)(2,1)}) %reduce-scatter.6.cloned.1.call-update) | async-done | bytes 147472 | tf_op jit(solution)/shard_map/reduce_scatter | solution.py:594
  409.3 11.5 %all_to_all.46 = bf16[4,32,576]{2,1,0:T(8,128)(2,1)S(1)} all-to-all(bf16[4,32,576]{2,1,0:T(8,128)(2,1)} %bitcast.125), channel_id=1, replica_groups=mesh['ctx'=8,'fsdp'=4] {'fsdp'}, dimensions={0} | all-to-all | bytes 294912 | tf_op jit(solution)/shard_map/all_to_all | solution.py:597
  420.8 3.5 all-to-all-start.3
  425.3 17.6 %all-to-all-done.3 = bf16[4,128,768]{2,1,0:T(8,128)(2,1)S(1)} async-done(((bf16[4,128,768]{2,1,0:T(8,128)(2,1)}), bf16[4,128,768]{2,1,0:T(8,128)(2,1)S(1)}, u32[]{:S(2)}, u32[]{:S(2)}) %all-to-all-start.3) | async-done | bytes 786464 | tf_op jit(solution)/shard_map/all_to_all | solution.py:590
  453.3 14.5 %all-gather.12.cloned.1.call-done = bf16[8,128,576]{1,2,0:T(8,128)(2,1)} async-done(((bf16[1,128,576]{1,2,0:T(8,128)(2,1)}), bf16[8,128,576]{1,2,0:T(8,128)(2,1)}) %all-gather.12.cloned.1.call-update) | async-done | bytes 1179664 | tf_op jit(solution)/shard_map/all_gather | solution.py:731
  477.8 2.9 reshape.400
  480.6 3.5 copy.115
  484.1 2.8 reshape.396
  (189 shorter events, 80.0 us)
Async XLA Ops:
  7.2 188.8 %copy-start = (bf16[768,768]{1,0:T(8,128)(2,1)S(1)}, bf16[768,768]{1,0:T(8,128)(2,1)}, u32[]{:S(2)}) copy-start(bf16[768,768]{1,0:T(8,128)(2,1)} %param.29) | copy-start | bytes 3538948
  7.2 6.2 %copy-start.11 = (bf16[192,2304]{1,0:T(8,128)(2,1)S(1)}, bf16[192,2304]{1,0:T(8,128)(2,1)}, u32[]{:S(2)}) copy-start(bf16[192,2304]{1,0:T(8,128)(2,1)} %param.20) | copy-start | bytes 2654212
  7.2 67.5 %all-gather.14.cloned.1.call-start = ((), (), s32[]{:S(2)}) async-start(), calls=%async_computation.16 | async-start | bytes 2088960 | tf_op jit(solution)/shard_map/all_gather | solution.py:606
  15.5 7.7 %copy-start.18 = (bf16[192]{0:T(256)(128)(2,1)S(1)}, bf16[192]{0:T(256)(128)(2,1)}, u32[]{:S(2)}) copy-start(bf16[192]{0:T(256)(128)(2,1)} %param.22) | copy-start | bytes 1156
  16.9 63.4 %all-to-all-start = ((bf16[4,192,576]{2,1,0:T(8,128)(2,1)}), bf16[4,192,576]{2,1,0:T(8,128)(2,1)}, u32[]{:S(2)}, u32[]{:S(2)}) async-start(bf16[4,192,576]{2,1,0:T(8,128)(2,1)} %copy.101), calls=%async_computation | async-start | bytes 1966080 | tf_op jit(solution)/shard_map/all_to_all | solution.py:597
  23.2 95.6 %all-gather.8.cloned.1.call-start = ((), (), s32[]{:S(2)}) async-start(), calls=%async_computation.10 | async-start | bytes 3538944 | tf_op jit(solution)/shard_map/all_gather | solution.py:631
  74.7 4.3 copy-start.2
  87.3 101.9 %all-gather.10.cloned.1.call-start = ((), (), s32[]{:S(2)}) async-start(), calls=%async_computation.11 | async-start | bytes 1474560 | tf_op jit(solution)/shard_map/all_gather | solution.py:587
  124.7 4.7 copy-start.19
  124.7 4.7 copy-start.17
  124.7 4.8 copy-start.16
  124.7 68.6 %all-to-all-start.1 = ((bf16[4,192,768]{2,1,0:T(8,128)(2,1)}), bf16[4,192,768]{2,1,0:T(8,128)(2,1)}, u32[]{:S(2)}, u32[]{:S(2)}) async-start(bf16[4,192,768]{2,1,0:T(8,128)(2,1)} %copy.105), calls=%async_computation.1 | async-start | bytes 2359296 | tf_op jit(solution)/shard_map/all_to_all | solution.py:597
  129.6 4.0 copy-start.20
  193.2 2.8 copy-start.12
  196.0 1.5 copy-start.21
  197.5 3.1 copy-start.4
  202.8 23.9 %all-to-all-start.2 = ((bf16[4,128,768]{2,1,0:T(8,128)(2,1)}), bf16[4,128,768]{2,1,0:T(8,128)(2,1)}, u32[]{:S(2)}, u32[]{:S(2)}) async-start(bf16[4,128,768]{2,1,0:T(8,128)(2,1)} %bitcast.117), calls=%async_computation.2 | async-start | bytes 1572864 | tf_op jit(solution)/shard_map/all_to_all | solution.py:590
  207.1 114.9 %reduce-scatter.4.cloned.1.call-start = ((), (), s32[]{:S(2)}) async-start(), calls=%async_computation.12 | async-start | bytes 3538944 | tf_op jit(solution)/shard_map/reduce_scatter | solution.py:594
  207.1 3.7 copy-start.13
  207.1 3.8 copy-start.22
  214.8 14.4 %copy-start.8 = (bf16[128,768]{1,0:T(8,128)(2,1)S(1)}, bf16[128,768]{1,0:T(8,128)(2,1)}, u32[]{:S(2)}) copy-start(bf16[128,768]{1,0:T(8,128)(2,1)} %param.31) | copy-start | bytes 589828
  229.2 19.2 %copy-start.9 = (bf16[192,512]{1,0:T(8,128)(2,1)S(1)}, bf16[192,512]{1,0:T(8,128)(2,1)}, u32[]{:S(2)}) copy-start(bf16[192,512]{1,0:T(8,128)(2,1)} %get-tuple-element.25) | copy-start | bytes 589828
  230.5 18.2 %copy-start.15 = (bf16[192,768]{1,0:T(8,128)(2,1)S(1)}, bf16[192,768]{1,0:T(8,128)(2,1)}, u32[]{:S(2)}) copy-start(bf16[192,768]{1,0:T(8,128)(2,1)} %param.23) | copy-start | bytes 884740
  248.3 1.6 copy-start.10
  276.7 91.7 %reduce-scatter.8.cloned.1.call-start = ((), (), s32[]{:S(2)}) async-start(), calls=%async_computation.15 | async-start | bytes 2985984 | tf_op jit(solution)/shard_map/reduce_scatter | solution.py:594
  325.1 24.8 %all-to-all-start.4 = ((bf16[4,128,768]{2,1,0:T(8,128)(2,1)}), bf16[4,128,768]{2,1,0:T(8,128)(2,1)S(1)}, u32[]{:S(2)}, u32[]{:S(2)}) async-start(bf16[4,128,768]{2,1,0:T(8,128)(2,1)} %bitcast.116), calls=%async_computation.5 | async-start | bytes 1572864 | tf_op jit(solution)/shard_map/all_to_all | solution.py:590
  329.9 79.4 %reduce-scatter.6.cloned.1.call-start = ((), (), s32[]{:S(2)}) async-start(), calls=%async_computation.13 | async-start | bytes 1474560 | tf_op jit(solution)/shard_map/reduce_scatter | solution.py:594
  370.0 10.8 %all-to-all-start.6 = ((bf16[4,24,768]{2,1,0:T(8,128)(2,1)}), bf16[4,24,768]{2,1,0:T(8,128)(2,1)S(1)}, u32[]{:S(2)}, u32[]{:S(2)}) async-start(bf16[4,24,768]{2,1,0:T(8,128)(2,1)} %bitcast.33), calls=%async_computation.9 | async-start | bytes 294912 | tf_op jit(solution)/shard_map/all_to_all | solution.py:597
  374.6 71.1 %all-gather.16.cloned.1.call-start = ((), (), s32[]{:S(2)}) async-start(), calls=%async_computation.17 | async-start | bytes 2985984 | tf_op jit(solution)/shard_map/all_gather | solution.py:679
  420.8 22.0 %all-to-all-start.3 = ((bf16[4,128,768]{2,1,0:T(8,128)(2,1)}), bf16[4,128,768]{2,1,0:T(8,128)(2,1)S(1)}, u32[]{:S(2)}, u32[]{:S(2)}) async-start(bf16[4,128,768]{2,1,0:T(8,128)(2,1)} %bitcast.16), calls=%async_computation.3 | async-start | bytes 1572864 | tf_op jit(solution)/shard_map/all_to_all | solution.py:590
  424.3 43.5 %all-gather.12.cloned.1.call-start = ((), (), s32[]{:S(2)}) async-start(), calls=%async_computation.14 | async-start | bytes 1327104 | tf_op jit(solution)/shard_map/all_gather | solution.py:731
  480.6 6.3 %copy-start.1 = (bf16[768,768]{1,0:T(8,128)(2,1)S(1)}, bf16[768,768]{1,0:T(8,128)(2,1)}, u32[]{:S(2)}) copy-start(bf16[768,768]{1,0:T(8,128)(2,1)} %param.29) | copy-start | bytes 3538948
  (5 other events, 5.8 us)
Sparse Core Ops, SparseCore 0:
  13.5 61.1 all-gather.13
  87.4 31.3 all-gather.7
  120.3 53.8 all-gather.9
  276.8 45.1 reduce-scatter.3
  325.4 43.0 reduce-scatter.7
  372.1 37.1 reduce-scatter.5
  411.8 30.1 all-gather.15
  443.8 23.9 all-gather.11
